TPU v7x, 32 devices: a whole 2x2x4 slice. The times are simulated.
32 devices in a mesh: ctx: 32 (over z, y, x, core).
Axes of the slice: x: 2, y: 2, z: 4, core: 2. Of those that a mesh axis runs over, the one named last changes fastest.
Arguments:
- queries: bfloat16 [4096, 2048], P('ctx'), may hold values from -128 to 128
- key_heads: bfloat16 [4096, 512], P('ctx'), may hold values from -8 to 8
- value_heads: bfloat16 [4096, 512], P('ctx'), may hold values from -6 to 6
- out_grad: bfloat16 [4096, 2048], P('ctx'), may hold values from -6 to 6
- segment: int32 [4096], P('ctx'), may hold values from 0 to 7, never falling along the last dimension, each value on 1 to 2048 neighbouring positions
- sink_logits: float32 [32], replicated, may hold values from 0 to 4
Outputs:
- query_grad: bfloat16 [4096, 2048], P('ctx')
- key_grad: bfloat16 [4096, 512], P('ctx')
- value_grad: bfloat16 [4096, 512], P('ctx')
- sink_grad: float32 [32], replicated
Inputs may be any that keep to these rules, and one draw needn't show every extreme that they name: `segment`: never falls along the tokens; each document holds 1 to 2048 tokens, one exactly that many.
All inputs are finite; a program needn't handle non-finite values.
Results may differ from a plain program's by a relative error of at most 0.008.
Values may be sent and summed in bfloat16 or wider, within the bound.
A program may use at most 128 MiB of HBM per device.

v0:
```python
import math

import jax
import jax.numpy as jnp
from jax import lax
from jax.sharding import PartitionSpec as P

QUERY_HEADS = 32
KV_HEADS = 8
HEAD_DIM = 64
WINDOW = 1024


def passed_along(block, axis, distance):
    devices = range(lax.axis_size(axis))
    route = [(i - distance, i) for i in devices if i - distance in devices]
    return lax.ppermute(block, axis, route)


def group_grads(query_group, key_group, value_group, grad_group, allowed, sink_group):
    score_scale = 1.0 / math.sqrt(HEAD_DIM)
    scores = (
        jnp.einsum("bgd,ld->gbl", query_group, key_group, preferred_element_type=jnp.float32)
        * score_scale
    )
    scores = jnp.where(allowed[None], scores, -jnp.inf)
    sink_grid = sink_group[:, None, None]
    top_value = jnp.maximum(jnp.max(scores, -1, keepdims=True), sink_grid)
    expd = jnp.exp(scores - top_value)
    sink_exp = jnp.exp(sink_grid - top_value)
    denom = jnp.sum(expd, -1, keepdims=True) + sink_exp
    probs = expd / denom
    sink_prob = (sink_exp / denom)[..., 0]
    weights = probs.astype(jnp.bfloat16)
    attended = jnp.einsum("gbl,ld->gbd", weights, value_group, preferred_element_type=jnp.float32)
    delta = jnp.einsum("bgd,gbd->gb", grad_group.astype(jnp.float32), attended)
    dprob = jnp.einsum("bgd,ld->gbl", grad_group, value_group, preferred_element_type=jnp.float32)
    dscore = (probs * (dprob - delta[..., None])).astype(jnp.bfloat16)
    query_part = (
        jnp.einsum("gbl,ld->bgd", dscore, key_group, preferred_element_type=jnp.float32)
        * score_scale
    )
    key_part = (
        jnp.einsum("gbl,bgd->ld", dscore, query_group, preferred_element_type=jnp.float32)
        * score_scale
    )
    value_part = jnp.einsum("gbl,bgd->ld", weights, grad_group, preferred_element_type=jnp.float32)
    sink_part = -jnp.sum(sink_prob * delta, -1)
    return (query_part, key_part, value_part, sink_part)


def per_device(queries, key_heads, value_heads, out_grad, segment, sink_logits):
    tok_rows = queries.shape[0]
    hop_count = WINDOW // tok_rows
    groups = QUERY_HEADS // KV_HEADS
    marked = segment + 1
    own_block = (key_heads, value_heads, marked)
    arrived = []
    current = own_block
    for distance in range(hop_count):
        current = passed_along((current[0], current[1], current[2]), "ctx", 1)
        arrived.append(current)
    ordered = arrived[::-1] + [own_block]
    key_all = jnp.concatenate([item[0] for item in ordered], 0)
    value_all = jnp.concatenate([item[1] for item in ordered], 0)
    marks_all = jnp.concatenate([item[2] for item in ordered], 0)
    key_span = key_all.shape[0]
    query_pos = jnp.arange(tok_rows, dtype=jnp.int32)[:, None]
    key_pos = jnp.arange(key_span, dtype=jnp.int32)[None, :]
    allowed = (
        (key_pos > query_pos)
        & (key_pos <= query_pos + WINDOW)
        & (marked[:, None] == marks_all[None, :])
    )
    query_list = []
    key_list = []
    value_list = []
    sink_list = []
    for kv_group in range(KV_HEADS):
        query_group = queries[
            :, kv_group * groups * HEAD_DIM : (kv_group + 1) * groups * HEAD_DIM
        ].reshape(tok_rows, groups, HEAD_DIM)
        grad_group = out_grad[
            :, kv_group * groups * HEAD_DIM : (kv_group + 1) * groups * HEAD_DIM
        ].reshape(tok_rows, groups, HEAD_DIM)
        key_group = key_all[:, kv_group * HEAD_DIM : (kv_group + 1) * HEAD_DIM]
        value_group = value_all[:, kv_group * HEAD_DIM : (kv_group + 1) * HEAD_DIM]
        sink_group = sink_logits[kv_group * groups : (kv_group + 1) * groups]
        query_part, key_part, value_part, sink_part = group_grads(
            query_group, key_group, value_group, grad_group, allowed, sink_group
        )
        query_list.append(query_part.reshape(tok_rows, groups * HEAD_DIM))
        key_list.append(key_part)
        value_list.append(value_part)
        sink_list.append(sink_part)
    query_grad = jnp.concatenate(query_list, 1).astype(jnp.bfloat16)
    key_partial = jnp.concatenate(key_list, 1)
    value_partial = jnp.concatenate(value_list, 1)
    sink_local = jnp.concatenate(sink_list, 0)

    def block_of(array, distance):
        first_row = (hop_count - distance) * tok_rows
        return array[first_row : first_row + tok_rows]

    running = (block_of(key_partial, hop_count), block_of(value_partial, hop_count))
    for distance in range(hop_count - 1, -1, -1):
        moved = passed_along((running[0], running[1]), "ctx", -1)
        running = (
            moved[0] + block_of(key_partial, distance),
            moved[1] + block_of(value_partial, distance),
        )
    key_sum, value_sum = running
    sink_grad = lax.psum(sink_local, "ctx")
    return (query_grad, key_sum.astype(jnp.bfloat16), value_sum.astype(jnp.bfloat16), sink_grad)


def solution(mesh):
    return jax.shard_map(
        per_device,
        mesh=mesh,
        in_specs=(P("ctx", None), P("ctx", None), P("ctx", None), P("ctx", None), P("ctx"), P()),
        out_specs=(P("ctx", None), P("ctx", None), P("ctx", None), P()),
        check_vma=False,
    )
```

profile of v0, /device:TPU:0, one launch (start us, length us, event | category | flops | bytes accessed | tf_op | source)
XLA Modules:
  0.0 265.1 jit_solution(11582177842661715491)
XLA Ops:
  1.3 2.5 collective-permute-start.8
  3.8 1.0 copy.13
  4.9 4.5 %collective-permute-start.16 = (bf16[128,512]{0,1:T(8,128)(2,1)S(1)}, bf16[128,512]{0,1:T(8,128)(2,1)S(1)}, u32[]{:S(2)}, u32[]{:S(2)}) collective-permute-start(bf16[128,512]{0,1:T(8,128)(2,1)S(1)} %copy.13), channel_id=1, source_target_pairs={{0,1},{1,2},{2,3},{3,4},{4,5},{5,6},{6,7},{7,8},{8,9},{9,10},{10,1... | collective-permute-start | bytes 393224 | tf_op jit(solution)/shard_map/ppermute | solution.py:17
  9.4 1.0 copy.10
  10.4 1.9 collective-permute-start
  12.3 3.5 %collective-permute-start.9 = (s32[128]{0:T(128)S(1)}, s32[128]{0:T(128)S(1)}, u32[]{:S(2)}, u32[]{:S(2)}) collective-permute-start(s32[128]{0:T(128)S(1)} %collective-permute-done.8), channel_id=1, source_target_pairs={{0,1},{1,2},{2,3},{3,4},{4,5},{5,6},{6,7},{7,8},{8,9},{9,10},{10,1... | collective-permute-start | bytes 1544 | tf_op jit(solution)/shard_map/ppermute | solution.py:17
  15.8 1.1 fusion.116
  17.0 1.9 collective-permute-start.10
  18.9 1.1 fusion.117
  20.0 3.7 %collective-permute-start.11 = (s32[128]{0:T(128)S(1)}, s32[128]{0:T(128)S(1)}, u32[]{:S(2)}, u32[]{:S(2)}) collective-permute-start(s32[128]{0:T(128)S(1)} %collective-permute-done.10), channel_id=1, source_target_pairs={{0,1},{1,2},{2,3},{3,4},{4,5},{5,6},{6,7},{7,8},{8,9},{9,10},{10,1... | collective-permute-start | bytes 1544 | tf_op jit(solution)/shard_map/ppermute | solution.py:17
  23.8 3.8 %collective-permute-start.1 = (bf16[128,512]{0,1:T(8,128)(2,1)S(1)}, bf16[128,512]{0,1:T(8,128)(2,1)S(1)}, u32[]{:S(2)}, u32[]{:S(2)}) collective-permute-start(bf16[128,512]{0,1:T(8,128)(2,1)S(1)} %collective-permute-done), channel_id=1, source_target_pairs={{0,1},{1,2},{2,3},{3,4},{4,5},{5,6},{6,7},{7,8},{8,9},{9,10},{10,1... | collective-permute-start | bytes 393224 | tf_op jit(solution)/shard_map/ppermute | solution.py:17
  28.2 2.6 collective-permute-start.12
  31.6 4.5 %collective-permute-start.13 = (s32[128]{0:T(128)S(1)}, s32[128]{0:T(128)S(1)}, u32[]{:S(2)}, u32[]{:S(2)}) collective-permute-start(s32[128]{0:T(128)S(1)} %collective-permute-done.12), channel_id=1, source_target_pairs={{0,1},{1,2},{2,3},{3,4},{4,5},{5,6},{6,7},{7,8},{8,9},{9,10},{10,1... | collective-permute-start | bytes 1544 | tf_op jit(solution)/shard_map/ppermute | solution.py:17
  36.9 4.1 %collective-permute-start.14 = (s32[128]{0:T(128)S(1)}, s32[128]{0:T(128)S(1)}, u32[]{:S(2)}, u32[]{:S(2)}) collective-permute-start(s32[128]{0:T(128)S(1)} %collective-permute-done.13), channel_id=1, source_target_pairs={{0,1},{1,2},{2,3},{3,4},{4,5},{5,6},{6,7},{7,8},{8,9},{9,10},{10,1... | collective-permute-start | bytes 1544 | tf_op jit(solution)/shard_map/ppermute | solution.py:17
  41.8 4.1 %collective-permute-start.15 = (s32[128]{0:T(128)S(1)}, s32[128]{0:T(128)S(1)}, u32[]{:S(2)}, u32[]{:S(2)}) collective-permute-start(s32[128]{0:T(128)S(1)} %collective-permute-done.14), channel_id=1, source_target_pairs={{0,1},{1,2},{2,3},{3,4},{4,5},{5,6},{6,7},{7,8},{8,9},{9,10},{10,1... | collective-permute-start | bytes 1544 | tf_op jit(solution)/shard_map/ppermute | solution.py:17
  46.2 4.2 %collective-permute-start.17 = (bf16[128,512]{0,1:T(8,128)(2,1)S(1)}, bf16[128,512]{0,1:T(8,128)(2,1)S(1)}, u32[]{:S(2)}, u32[]{:S(2)}) collective-permute-start(bf16[128,512]{0,1:T(8,128)(2,1)S(1)} %collective-permute-done.16), channel_id=1, source_target_pairs={{0,1},{1,2},{2,3},{3,4},{4,5},{5,6},{6,7},{7,8},{8,9},{9,10},{10,1... | collective-permute-start | bytes 393224 | tf_op jit(solution)/shard_map/ppermute | solution.py:17
  50.4 2.7 %collective-permute-start.2 = (bf16[128,512]{0,1:T(8,128)(2,1)S(1)}, bf16[128,512]{0,1:T(8,128)(2,1)S(1)}, u32[]{:S(2)}, u32[]{:S(2)}) collective-permute-start(bf16[128,512]{0,1:T(8,128)(2,1)S(1)} %collective-permute-done.1), channel_id=1, source_target_pairs={{0,1},{1,2},{2,3},{3,4},{4,5},{5,6},{6,7},{7,8},{8,9},{9,10},{10,1... | collective-permute-start | bytes 393224 | tf_op jit(solution)/shard_map/ppermute | solution.py:17
  53.2 5.1 %collective-permute-start.18 = (bf16[128,512]{0,1:T(8,128)(2,1)S(1)}, bf16[128,512]{0,1:T(8,128)(2,1)S(1)}, u32[]{:S(2)}, u32[]{:S(2)}) collective-permute-start(bf16[128,512]{0,1:T(8,128)(2,1)S(1)} %collective-permute-done.17), channel_id=1, source_target_pairs={{0,1},{1,2},{2,3},{3,4},{4,5},{5,6},{6,7},{7,8},{8,9},{9,10},{10,1... | collective-permute-start | bytes 393224 | tf_op jit(solution)/shard_map/ppermute | solution.py:17
  58.3 1.9 collective-permute-start.3
  60.3 4.3 %collective-permute-start.19 = (bf16[128,512]{0,1:T(8,128)(2,1)S(1)}, bf16[128,512]{0,1:T(8,128)(2,1)S(1)}, u32[]{:S(2)}, u32[]{:S(2)}) collective-permute-start(bf16[128,512]{0,1:T(8,128)(2,1)S(1)} %collective-permute-done.18), channel_id=1, source_target_pairs={{0,1},{1,2},{2,3},{3,4},{4,5},{5,6},{6,7},{7,8},{8,9},{9,10},{10,1... | collective-permute-start | bytes 393224 | tf_op jit(solution)/shard_map/ppermute | solution.py:17
  64.6 4.1 %collective-permute-start.4 = (bf16[128,512]{0,1:T(8,128)(2,1)S(1)}, bf16[128,512]{0,1:T(8,128)(2,1)S(1)}, u32[]{:S(2)}, u32[]{:S(2)}) collective-permute-start(bf16[128,512]{0,1:T(8,128)(2,1)S(1)} %collective-permute-done.3), channel_id=1, source_target_pairs={{0,1},{1,2},{2,3},{3,4},{4,5},{5,6},{6,7},{7,8},{8,9},{9,10},{10,1... | collective-permute-start | bytes 393224 | tf_op jit(solution)/shard_map/ppermute | solution.py:17
  68.7 6.0 %collective-permute-start.20 = (bf16[128,512]{0,1:T(8,128)(2,1)S(1)}, bf16[128,512]{0,1:T(8,128)(2,1)S(1)}, u32[]{:S(2)}, u32[]{:S(2)}) collective-permute-start(bf16[128,512]{0,1:T(8,128)(2,1)S(1)} %collective-permute-done.19), channel_id=1, source_target_pairs={{0,1},{1,2},{2,3},{3,4},{4,5},{5,6},{6,7},{7,8},{8,9},{9,10},{10,1... | collective-permute-start | bytes 393224 | tf_op jit(solution)/shard_map/ppermute | solution.py:17
  74.7 1.9 collective-permute-start.5
  76.6 5.2 %collective-permute-start.21 = (bf16[128,512]{0,1:T(8,128)(2,1)S(1)}, bf16[128,512]{0,1:T(8,128)(2,1)S(1)}, u32[]{:S(2)}, u32[]{:S(2)}) collective-permute-start(bf16[128,512]{0,1:T(8,128)(2,1)S(1)} %collective-permute-done.20), channel_id=1, source_target_pairs={{0,1},{1,2},{2,3},{3,4},{4,5},{5,6},{6,7},{7,8},{8,9},{9,10},{10,1... | collective-permute-start | bytes 393224 | tf_op jit(solution)/shard_map/ppermute | solution.py:17
  81.9 2.8 %collective-permute-start.6 = (bf16[128,512]{0,1:T(8,128)(2,1)S(1)}, bf16[128,512]{0,1:T(8,128)(2,1)S(1)}, u32[]{:S(2)}, u32[]{:S(2)}) collective-permute-start(bf16[128,512]{0,1:T(8,128)(2,1)S(1)} %collective-permute-done.5), channel_id=1, source_target_pairs={{0,1},{1,2},{2,3},{3,4},{4,5},{5,6},{6,7},{7,8},{8,9},{9,10},{10,1... | collective-permute-start | bytes 393224 | tf_op jit(solution)/shard_map/ppermute | solution.py:17
  84.7 4.3 %collective-permute-start.22 = (bf16[128,512]{0,1:T(8,128)(2,1)S(1)}, bf16[128,512]{0,1:T(8,128)(2,1)S(1)}, u32[]{:S(2)}, u32[]{:S(2)}) collective-permute-start(bf16[128,512]{0,1:T(8,128)(2,1)S(1)} %collective-permute-done.21), channel_id=1, source_target_pairs={{0,1},{1,2},{2,3},{3,4},{4,5},{5,6},{6,7},{7,8},{8,9},{9,10},{10,1... | collective-permute-start | bytes 393224 | tf_op jit(solution)/shard_map/ppermute | solution.py:17
  89.0 3.7 %collective-permute-start.7 = (bf16[128,512]{0,1:T(8,128)(2,1)S(1)}, bf16[128,512]{0,1:T(8,128)(2,1)S(1)}, u32[]{:S(2)}, u32[]{:S(2)}) collective-permute-start(bf16[128,512]{0,1:T(8,128)(2,1)S(1)} %collective-permute-done.6), channel_id=1, source_target_pairs={{0,1},{1,2},{2,3},{3,4},{4,5},{5,6},{6,7},{7,8},{8,9},{9,10},{10,1... | collective-permute-start | bytes 393224 | tf_op jit(solution)/shard_map/ppermute | solution.py:17
  93.0 3.6 %collective-permute-start.23 = (bf16[128,512]{0,1:T(8,128)(2,1)S(1)}, bf16[128,512]{0,1:T(8,128)(2,1)S(1)}, u32[]{:S(2)}, u32[]{:S(2)}) collective-permute-start(bf16[128,512]{0,1:T(8,128)(2,1)S(1)} %collective-permute-done.22), channel_id=1, source_target_pairs={{0,1},{1,2},{2,3},{3,4},{4,5},{5,6},{6,7},{7,8},{8,9},{9,10},{10,1... | collective-permute-start | bytes 393224 | tf_op jit(solution)/shard_map/ppermute | solution.py:17
  115.1 1.2 fusion.84
  129.3 1.3 collective-permute-start.24
  135.7 1.3 collective-permute-start.32
  139.2 1.0 slice_add_fusion.15
  140.2 1.3 collective-permute-start.25
  141.5 1.6 collective-permute-done.32
  143.8 1.3 collective-permute-start.33
  145.1 1.5 constant_dynamic-update-slice_fusion.25
  148.0 1.0 slice_add_fusion.14
  149.0 1.3 collective-permute-start.26
  150.3 2.2 collective-permute-done.33
  152.5 1.3 collective-permute-start.34
  153.8 1.5 constant_dynamic-update-slice_fusion.24
  155.3 1.6 copy.41
  157.4 1.0 slice_add_fusion.13
  158.4 1.3 collective-permute-start.27
  160.2 1.3 collective-permute-start.35
  161.5 1.5 constant_dynamic-update-slice_fusion.23
  163.0 1.6 copy.42
  164.5 1.6 collective-permute-done.27
  167.2 1.3 collective-permute-start.28
  168.5 1.3 collective-permute-start.36
  169.8 1.5 constant_dynamic-update-slice_fusion.22
  171.3 1.6 copy.43
  172.9 2.0 collective-permute-done.28
  175.8 1.3 collective-permute-start.29
  177.2 1.3 collective-permute-start.37
  178.5 1.5 constant_dynamic-update-slice_fusion.21
  180.7 2.8 %collective-permute-done.29 = f32[128,512]{0,1:T(8,128)S(1)} collective-permute-done((f32[128,512]{0,1:T(8,128)S(1)}, f32[128,512]{0,1:T(8,128)S(1)}, u32[]{:S(2)}, u32[]{:S(2)}) %collective-permute-start.29) | collective-permute-done | bytes 262176 | tf_op jit(solution)/shard_map/ppermute | solution.py:17
  184.5 1.3 collective-permute-start.30
  186.8 1.3 collective-permute-start.38
  188.1 1.5 constant_dynamic-update-slice_fusion.20
  193.6 1.3 collective-permute-start.31
  195.5 1.3 collective-permute-start.39
  197.5 65.0 %psum.7 = f32[32]{0:T(128)} all-reduce(f32[32]{0:T(128)S(1)} %concatenate.28), channel_id=1, replica_groups=mesh['ctx'=32] {'ctx'}, use_global_device_ids=true, to_apply=%region_24.25 | all-reduce | flops 32 | bytes 256 | tf_op jit(solution)/shard_map/psum | solution.py:113
  262.5 1.1 fusion.107
  (242 shorter events, 57.2 us)
Async XLA Ops:
  0.6 26.9 %copy-start.3 = (f32[32]{0:T(128)S(1)}, f32[32]{0:T(128)}, u32[]{:S(2)}) copy-start(f32[32]{0:T(128)} %param.11) | copy-start | bytes 388
  1.3 83.4 %copy-start.21 = (s32[128]{0:T(128)S(1)}, s32[128]{0:T(128)}, u32[]{:S(2)}) copy-start(s32[128]{0:T(128)} %param.10) | copy-start | bytes 1540
  1.3 11.0 %collective-permute-start.8 = (s32[128]{0:T(128)S(1)}, s32[128]{0:T(128)S(1)}, u32[]{:S(2)}, u32[]{:S(2)}) collective-permute-start(s32[128]{0:T(128)S(1)} %broadcast_add_fusion), channel_id=1, source_target_pairs={{0,1},{1,2},{2,3},{3,4},{4,5},{5,6},{6,7},{7,8},{8,9},{9,10},{10,1... | collective-permute-start | bytes 1544 | tf_op jit(solution)/shard_map/ppermute | solution.py:17
  4.9 41.4 %collective-permute-start.16 = (bf16[128,512]{0,1:T(8,128)(2,1)S(1)}, bf16[128,512]{0,1:T(8,128)(2,1)S(1)}, u32[]{:S(2)}, u32[]{:S(2)}) collective-permute-start(bf16[128,512]{0,1:T(8,128)(2,1)S(1)} %copy.13), channel_id=1, source_target_pairs={{0,1},{1,2},{2,3},{3,4},{4,5},{5,6},{6,7},{7,8},{8,9},{9,10},{10,1... | collective-permute-start | bytes 393224 | tf_op jit(solution)/shard_map/ppermute | solution.py:17
  10.4 13.4 %collective-permute-start = (bf16[128,512]{0,1:T(8,128)(2,1)S(1)}, bf16[128,512]{0,1:T(8,128)(2,1)S(1)}, u32[]{:S(2)}, u32[]{:S(2)}) collective-permute-start(bf16[128,512]{0,1:T(8,128)(2,1)S(1)} %copy.10), channel_id=1, source_target_pairs={{0,1},{1,2},{2,3},{3,4},{4,5},{5,6},{6,7},{7,8},{8,9},{9,10},{10,1... | collective-permute-start | bytes 393224 | tf_op jit(solution)/shard_map/ppermute | solution.py:17
  12.3 4.6 %collective-permute-start.9 = (s32[128]{0:T(128)S(1)}, s32[128]{0:T(128)S(1)}, u32[]{:S(2)}, u32[]{:S(2)}) collective-permute-start(s32[128]{0:T(128)S(1)} %collective-permute-done.8), channel_id=1, source_target_pairs={{0,1},{1,2},{2,3},{3,4},{4,5},{5,6},{6,7},{7,8},{8,9},{9,10},{10,1... | collective-permute-start | bytes 1544 | tf_op jit(solution)/shard_map/ppermute | solution.py:17
  17.0 3.0 %collective-permute-start.10 = (s32[128]{0:T(128)S(1)}, s32[128]{0:T(128)S(1)}, u32[]{:S(2)}, u32[]{:S(2)}) collective-permute-start(s32[128]{0:T(128)S(1)} %collective-permute-done.9), channel_id=1, source_target_pairs={{0,1},{1,2},{2,3},{3,4},{4,5},{5,6},{6,7},{7,8},{8,9},{9,10},{10,1... | collective-permute-start | bytes 1544 | tf_op jit(solution)/shard_map/ppermute | solution.py:17
  20.0 8.2 %collective-permute-start.11 = (s32[128]{0:T(128)S(1)}, s32[128]{0:T(128)S(1)}, u32[]{:S(2)}, u32[]{:S(2)}) collective-permute-start(s32[128]{0:T(128)S(1)} %collective-permute-done.10), channel_id=1, source_target_pairs={{0,1},{1,2},{2,3},{3,4},{4,5},{5,6},{6,7},{7,8},{8,9},{9,10},{10,1... | collective-permute-start | bytes 1544 | tf_op jit(solution)/shard_map/ppermute | solution.py:17
  23.8 26.6 %collective-permute-start.1 = (bf16[128,512]{0,1:T(8,128)(2,1)S(1)}, bf16[128,512]{0,1:T(8,128)(2,1)S(1)}, u32[]{:S(2)}, u32[]{:S(2)}) collective-permute-start(bf16[128,512]{0,1:T(8,128)(2,1)S(1)} %collective-permute-done), channel_id=1, source_target_pairs={{0,1},{1,2},{2,3},{3,4},{4,5},{5,6},{6,7},{7,8},{8,9},{9,10},{10,1... | collective-permute-start | bytes 393224 | tf_op jit(solution)/shard_map/ppermute | solution.py:17
  28.2 70.5 %copy-start.10 = (f32[4]{0:T(128)}, f32[4]{0:T(128)S(1)}, u32[]{:S(2)}) copy-start(f32[4]{0:T(128)S(1)} %get-tuple-element.30) | copy-start | bytes 52
  28.2 89.0 %copy-start.12 = (f32[4]{0:T(128)}, f32[4]{0:T(128)S(1)}, u32[]{:S(2)}) copy-start(f32[4]{0:T(128)S(1)} %get-tuple-element.27) | copy-start | bytes 52
  28.2 3.4 %collective-permute-start.12 = (s32[128]{0:T(128)S(1)}, s32[128]{0:T(128)S(1)}, u32[]{:S(2)}, u32[]{:S(2)}) collective-permute-start(s32[128]{0:T(128)S(1)} %collective-permute-done.11), channel_id=1, source_target_pairs={{0,1},{1,2},{2,3},{3,4},{4,5},{5,6},{6,7},{7,8},{8,9},{9,10},{10,1... | collective-permute-start | bytes 1544 | tf_op jit(solution)/shard_map/ppermute | solution.py:17
  31.6 5.3 %collective-permute-start.13 = (s32[128]{0:T(128)S(1)}, s32[128]{0:T(128)S(1)}, u32[]{:S(2)}, u32[]{:S(2)}) collective-permute-start(s32[128]{0:T(128)S(1)} %collective-permute-done.12), channel_id=1, source_target_pairs={{0,1},{1,2},{2,3},{3,4},{4,5},{5,6},{6,7},{7,8},{8,9},{9,10},{10,1... | collective-permute-start | bytes 1544 | tf_op jit(solution)/shard_map/ppermute | solution.py:17
  36.9 4.9 %collective-permute-start.14 = (s32[128]{0:T(128)S(1)}, s32[128]{0:T(128)S(1)}, u32[]{:S(2)}, u32[]{:S(2)}) collective-permute-start(s32[128]{0:T(128)S(1)} %collective-permute-done.13), channel_id=1, source_target_pairs={{0,1},{1,2},{2,3},{3,4},{4,5},{5,6},{6,7},{7,8},{8,9},{9,10},{10,1... | collective-permute-start | bytes 1544 | tf_op jit(solution)/shard_map/ppermute | solution.py:17
  41.8 11.4 %collective-permute-start.15 = (s32[128]{0:T(128)S(1)}, s32[128]{0:T(128)S(1)}, u32[]{:S(2)}, u32[]{:S(2)}) collective-permute-start(s32[128]{0:T(128)S(1)} %collective-permute-done.14), channel_id=1, source_target_pairs={{0,1},{1,2},{2,3},{3,4},{4,5},{5,6},{6,7},{7,8},{8,9},{9,10},{10,1... | collective-permute-start | bytes 1544 | tf_op jit(solution)/shard_map/ppermute | solution.py:17
  46.2 7.0 %collective-permute-start.17 = (bf16[128,512]{0,1:T(8,128)(2,1)S(1)}, bf16[128,512]{0,1:T(8,128)(2,1)S(1)}, u32[]{:S(2)}, u32[]{:S(2)}) collective-permute-start(bf16[128,512]{0,1:T(8,128)(2,1)S(1)} %collective-permute-done.16), channel_id=1, source_target_pairs={{0,1},{1,2},{2,3},{3,4},{4,5},{5,6},{6,7},{7,8},{8,9},{9,10},{10,1... | collective-permute-start | bytes 393224 | tf_op jit(solution)/shard_map/ppermute | solution.py:17
  50.4 7.9 %collective-permute-start.2 = (bf16[128,512]{0,1:T(8,128)(2,1)S(1)}, bf16[128,512]{0,1:T(8,128)(2,1)S(1)}, u32[]{:S(2)}, u32[]{:S(2)}) collective-permute-start(bf16[128,512]{0,1:T(8,128)(2,1)S(1)} %collective-permute-done.1), channel_id=1, source_target_pairs={{0,1},{1,2},{2,3},{3,4},{4,5},{5,6},{6,7},{7,8},{8,9},{9,10},{10,1... | collective-permute-start | bytes 393224 | tf_op jit(solution)/shard_map/ppermute | solution.py:17
  53.2 7.1 %collective-permute-start.18 = (bf16[128,512]{0,1:T(8,128)(2,1)S(1)}, bf16[128,512]{0,1:T(8,128)(2,1)S(1)}, u32[]{:S(2)}, u32[]{:S(2)}) collective-permute-start(bf16[128,512]{0,1:T(8,128)(2,1)S(1)} %collective-permute-done.17), channel_id=1, source_target_pairs={{0,1},{1,2},{2,3},{3,4},{4,5},{5,6},{6,7},{7,8},{8,9},{9,10},{10,1... | collective-permute-start | bytes 393224 | tf_op jit(solution)/shard_map/ppermute | solution.py:17
  58.3 6.3 %collective-permute-start.3 = (bf16[128,512]{0,1:T(8,128)(2,1)S(1)}, bf16[128,512]{0,1:T(8,128)(2,1)S(1)}, u32[]{:S(2)}, u32[]{:S(2)}) collective-permute-start(bf16[128,512]{0,1:T(8,128)(2,1)S(1)} %collective-permute-done.2), channel_id=1, source_target_pairs={{0,1},{1,2},{2,3},{3,4},{4,5},{5,6},{6,7},{7,8},{8,9},{9,10},{10,1... | collective-permute-start | bytes 393224 | tf_op jit(solution)/shard_map/ppermute | solution.py:17
  60.3 8.4 %collective-permute-start.19 = (bf16[128,512]{0,1:T(8,128)(2,1)S(1)}, bf16[128,512]{0,1:T(8,128)(2,1)S(1)}, u32[]{:S(2)}, u32[]{:S(2)}) collective-permute-start(bf16[128,512]{0,1:T(8,128)(2,1)S(1)} %collective-permute-done.18), channel_id=1, source_target_pairs={{0,1},{1,2},{2,3},{3,4},{4,5},{5,6},{6,7},{7,8},{8,9},{9,10},{10,1... | collective-permute-start | bytes 393224 | tf_op jit(solution)/shard_map/ppermute | solution.py:17
  64.6 10.1 %collective-permute-start.4 = (bf16[128,512]{0,1:T(8,128)(2,1)S(1)}, bf16[128,512]{0,1:T(8,128)(2,1)S(1)}, u32[]{:S(2)}, u32[]{:S(2)}) collective-permute-start(bf16[128,512]{0,1:T(8,128)(2,1)S(1)} %collective-permute-done.3), channel_id=1, source_target_pairs={{0,1},{1,2},{2,3},{3,4},{4,5},{5,6},{6,7},{7,8},{8,9},{9,10},{10,1... | collective-permute-start | bytes 393224 | tf_op jit(solution)/shard_map/ppermute | solution.py:17
  68.7 8.0 %collective-permute-start.20 = (bf16[128,512]{0,1:T(8,128)(2,1)S(1)}, bf16[128,512]{0,1:T(8,128)(2,1)S(1)}, u32[]{:S(2)}, u32[]{:S(2)}) collective-permute-start(bf16[128,512]{0,1:T(8,128)(2,1)S(1)} %collective-permute-done.19), channel_id=1, source_target_pairs={{0,1},{1,2},{2,3},{3,4},{4,5},{5,6},{6,7},{7,8},{8,9},{9,10},{10,1... | collective-permute-start | bytes 393224 | tf_op jit(solution)/shard_map/ppermute | solution.py:17
  74.7 7.2 %collective-permute-start.5 = (bf16[128,512]{0,1:T(8,128)(2,1)S(1)}, bf16[128,512]{0,1:T(8,128)(2,1)S(1)}, u32[]{:S(2)}, u32[]{:S(2)}) collective-permute-start(bf16[128,512]{0,1:T(8,128)(2,1)S(1)} %collective-permute-done.4), channel_id=1, source_target_pairs={{0,1},{1,2},{2,3},{3,4},{4,5},{5,6},{6,7},{7,8},{8,9},{9,10},{10,1... | collective-permute-start | bytes 393224 | tf_op jit(solution)/shard_map/ppermute | solution.py:17
  76.6 8.1 %collective-permute-start.21 = (bf16[128,512]{0,1:T(8,128)(2,1)S(1)}, bf16[128,512]{0,1:T(8,128)(2,1)S(1)}, u32[]{:S(2)}, u32[]{:S(2)}) collective-permute-start(bf16[128,512]{0,1:T(8,128)(2,1)S(1)} %collective-permute-done.20), channel_id=1, source_target_pairs={{0,1},{1,2},{2,3},{3,4},{4,5},{5,6},{6,7},{7,8},{8,9},{9,10},{10,1... | collective-permute-start | bytes 393224 | tf_op jit(solution)/shard_map/ppermute | solution.py:17
  81.9 7.2 %collective-permute-start.6 = (bf16[128,512]{0,1:T(8,128)(2,1)S(1)}, bf16[128,512]{0,1:T(8,128)(2,1)S(1)}, u32[]{:S(2)}, u32[]{:S(2)}) collective-permute-start(bf16[128,512]{0,1:T(8,128)(2,1)S(1)} %collective-permute-done.5), channel_id=1, source_target_pairs={{0,1},{1,2},{2,3},{3,4},{4,5},{5,6},{6,7},{7,8},{8,9},{9,10},{10,1... | collective-permute-start | bytes 393224 | tf_op jit(solution)/shard_map/ppermute | solution.py:17
  84.7 8.3 %collective-permute-start.22 = (bf16[128,512]{0,1:T(8,128)(2,1)S(1)}, bf16[128,512]{0,1:T(8,128)(2,1)S(1)}, u32[]{:S(2)}, u32[]{:S(2)}) collective-permute-start(bf16[128,512]{0,1:T(8,128)(2,1)S(1)} %collective-permute-done.21), channel_id=1, source_target_pairs={{0,1},{1,2},{2,3},{3,4},{4,5},{5,6},{6,7},{7,8},{8,9},{9,10},{10,1... | collective-permute-start | bytes 393224 | tf_op jit(solution)/shard_map/ppermute | solution.py:17
  89.0 7.6 %collective-permute-start.7 = (bf16[128,512]{0,1:T(8,128)(2,1)S(1)}, bf16[128,512]{0,1:T(8,128)(2,1)S(1)}, u32[]{:S(2)}, u32[]{:S(2)}) collective-permute-start(bf16[128,512]{0,1:T(8,128)(2,1)S(1)} %collective-permute-done.6), channel_id=1, source_target_pairs={{0,1},{1,2},{2,3},{3,4},{4,5},{5,6},{6,7},{7,8},{8,9},{9,10},{10,1... | collective-permute-start | bytes 393224 | tf_op jit(solution)/shard_map/ppermute | solution.py:17
  93.0 4.4 %collective-permute-start.23 = (bf16[128,512]{0,1:T(8,128)(2,1)S(1)}, bf16[128,512]{0,1:T(8,128)(2,1)S(1)}, u32[]{:S(2)}, u32[]{:S(2)}) collective-permute-start(bf16[128,512]{0,1:T(8,128)(2,1)S(1)} %collective-permute-done.22), channel_id=1, source_target_pairs={{0,1},{1,2},{2,3},{3,4},{4,5},{5,6},{6,7},{7,8},{8,9},{9,10},{10,1... | collective-permute-start | bytes 393224 | tf_op jit(solution)/shard_map/ppermute | solution.py:17
  99.5 0.7 copy-start.4
  108.0 0.9 copy-start.15
  110.8 1.5 copy-start.16
  118.7 1.5 copy-start.14
  122.1 0.9 copy-start.8
  124.2 0.7 copy-start.6
  129.3 2.8 %copy-start = (f32[1152,512]{0,1:T(8,128)}, f32[1152,512]{0,1:T(8,128)S(1)}, u32[]{:S(2)}) copy-start(f32[1152,512]{0,1:T(8,128)S(1)} %fusion.49) | copy-start | bytes 7077892
  129.3 9.9 %collective-permute-start.24 = (f32[128,512]{0,1:T(8,128)S(1)}, f32[128,512]{0,1:T(8,128)S(1)}, u32[]{:S(2)}, u32[]{:S(2)}) collective-permute-start(f32[128,512]{0,1:T(8,128)S(1)} %slice.248), channel_id=1, source_target_pairs={{1,0},{2,1},{3,2},{4,3},{5,4},{6,5},{7,6},{8,7},{9,8},{10,9},{11,1... | collective-permute-start | bytes 786440 | tf_op jit(solution)/shard_map/ppermute | solution.py:17
  132.5 1.5 copy-start.13
  132.5 2.3 copy-start.1
  132.5 4.4 %copy-start.5 = (f32[4,128]{1,0:T(4,128)S(1)}, f32[4,128]{1,0:T(4,128)}, u32[]{:S(2)}) copy-start(f32[4,128]{1,0:T(4,128)} %copy-done.4) | copy-start | bytes 6148
  132.6 4.4 %copy-start.7 = (f32[4,128]{1,0:T(4,128)S(1)}, f32[4,128]{1,0:T(4,128)}, u32[]{:S(2)}) copy-start(f32[4,128]{1,0:T(4,128)} %copy-done.6) | copy-start | bytes 6148
  132.6 4.4 %copy-start.9 = (f32[4]{0:T(128)S(1)}, f32[4]{0:T(128)}, u32[]{:S(2)}) copy-start(f32[4]{0:T(128)} %get-tuple-element.29) | copy-start | bytes 52
  132.6 4.4 %copy-start.11 = (f32[4]{0:T(128)S(1)}, f32[4]{0:T(128)}, u32[]{:S(2)}) copy-start(f32[4]{0:T(128)} %copy-done.10) | copy-start | bytes 52
  132.6 5.8 %copy-start.2 = (bf16[64,4,128]{2,0,1:T(8,128)(2,1)S(1)}, bf16[64,4,128]{2,0,1:T(8,128)(2,1)}, u32[]{:S(2)}) copy-start(bf16[64,4,128]{2,0,1:T(8,128)(2,1)} %fusion.81) | copy-start | bytes 196612
  135.7 7.4 %collective-permute-start.32 = (f32[128,512]{0,1:T(8,128)}, f32[128,512]{0,1:T(8,128)S(1)}, u32[]{:S(2)}, u32[]{:S(2)}) collective-permute-start(f32[128,512]{0,1:T(8,128)} %slice.257), channel_id=1, source_target_pairs={{1,0},{2,1},{3,2},{4,3},{5,4},{6,5},{7,6},{8,7},{9,8},{10,9},{11,1... | collective-permute-start | bytes 786440 | tf_op jit(solution)/shard_map/ppermute | solution.py:17
  140.2 7.8 %collective-permute-start.25 = (f32[128,512]{0,1:T(8,128)S(1)}, f32[128,512]{0,1:T(8,128)S(1)}, u32[]{:S(2)}, u32[]{:S(2)}) collective-permute-start(f32[128,512]{0,1:T(8,128)S(1)} %slice_add_fusion.15), channel_id=1, source_target_pairs={{1,0},{2,1},{3,2},{4,3},{5,4},{6,5},{7,6},{8,7},{9,8},{10,9},{11,1... | collective-permute-start | bytes 786440 | tf_op jit(solution)/shard_map/ppermute | solution.py:17
  143.8 8.6 %collective-permute-start.33 = (f32[128,512]{0,1:T(8,128)}, f32[128,512]{0,1:T(8,128)S(1)}, u32[]{:S(2)}, u32[]{:S(2)}) collective-permute-start(f32[128,512]{0,1:T(8,128)} %slice_add_fusion.7), channel_id=1, source_target_pairs={{1,0},{2,1},{3,2},{4,3},{5,4},{6,5},{7,6},{8,7},{9,8},{10,9},{11,1... | collective-permute-start | bytes 786440 | tf_op jit(solution)/shard_map/ppermute | solution.py:17
  149.0 8.4 %collective-permute-start.26 = (f32[128,512]{0,1:T(8,128)S(1)}, f32[128,512]{0,1:T(8,128)S(1)}, u32[]{:S(2)}, u32[]{:S(2)}) collective-permute-start(f32[128,512]{0,1:T(8,128)S(1)} %slice_add_fusion.14), channel_id=1, source_target_pairs={{1,0},{2,1},{3,2},{4,3},{5,4},{6,5},{7,6},{8,7},{9,8},{10,9},{11,1... | collective-permute-start | bytes 786440 | tf_op jit(solution)/shard_map/ppermute | solution.py:17
  152.5 7.7 %collective-permute-start.34 = (f32[128,512]{0,1:T(8,128)S(1)}, f32[128,512]{0,1:T(8,128)S(1)}, u32[]{:S(2)}, u32[]{:S(2)}) collective-permute-start(f32[128,512]{0,1:T(8,128)S(1)} %slice_add_fusion.6), channel_id=1, source_target_pairs={{1,0},{2,1},{3,2},{4,3},{5,4},{6,5},{7,6},{8,7},{9,8},{10,9},{11,1... | collective-permute-start | bytes 786440 | tf_op jit(solution)/shard_map/ppermute | solution.py:17
  158.4 7.7 %collective-permute-start.27 = (f32[128,512]{0,1:T(8,128)S(1)}, f32[128,512]{0,1:T(8,128)S(1)}, u32[]{:S(2)}, u32[]{:S(2)}) collective-permute-start(f32[128,512]{0,1:T(8,128)S(1)} %slice_add_fusion.13), channel_id=1, source_target_pairs={{1,0},{2,1},{3,2},{4,3},{5,4},{6,5},{7,6},{8,7},{9,8},{10,9},{11,1... | collective-permute-start | bytes 786440 | tf_op jit(solution)/shard_map/ppermute | solution.py:17
  160.2 8.3 %collective-permute-start.35 = (f32[128,512]{0,1:T(8,128)S(1)}, f32[128,512]{0,1:T(8,128)S(1)}, u32[]{:S(2)}, u32[]{:S(2)}) collective-permute-start(f32[128,512]{0,1:T(8,128)S(1)} %slice_add_fusion.5), channel_id=1, source_target_pairs={{1,0},{2,1},{3,2},{4,3},{5,4},{6,5},{7,6},{8,7},{9,8},{10,9},{11,1... | collective-permute-start | bytes 786440 | tf_op jit(solution)/shard_map/ppermute | solution.py:17
  167.1 22.6 %copy-start.18 = (f32[4]{0:T(128)S(1)}, f32[4]{0:T(128)}, u32[]{:S(2)}) copy-start(f32[4]{0:T(128)} %get-tuple-element.48) | copy-start | bytes 52
  167.1 22.6 %copy-start.17 = (f32[4]{0:T(128)S(1)}, f32[4]{0:T(128)}, u32[]{:S(2)}) copy-start(f32[4]{0:T(128)} %get-tuple-element.49) | copy-start | bytes 52
  167.1 22.6 %copy-start.20 = (f32[4]{0:T(128)S(1)}, f32[4]{0:T(128)}, u32[]{:S(2)}) copy-start(f32[4]{0:T(128)} %get-tuple-element.50) | copy-start | bytes 52
  167.1 22.6 %copy-start.19 = (f32[4]{0:T(128)S(1)}, f32[4]{0:T(128)}, u32[]{:S(2)}) copy-start(f32[4]{0:T(128)} %get-tuple-element.51) | copy-start | bytes 52
  167.2 7.7 %collective-permute-start.28 = (f32[128,512]{0,1:T(8,128)S(1)}, f32[128,512]{0,1:T(8,128)S(1)}, u32[]{:S(2)}, u32[]{:S(2)}) collective-permute-start(f32[128,512]{0,1:T(8,128)S(1)} %slice_add_fusion.12), channel_id=1, source_target_pairs={{1,0},{2,1},{3,2},{4,3},{5,4},{6,5},{7,6},{8,7},{9,8},{10,9},{11,1... | collective-permute-start | bytes 786440 | tf_op jit(solution)/shard_map/ppermute | solution.py:17
  168.5 8.6 %collective-permute-start.36 = (f32[128,512]{0,1:T(8,128)S(1)}, f32[128,512]{0,1:T(8,128)S(1)}, u32[]{:S(2)}, u32[]{:S(2)}) collective-permute-start(f32[128,512]{0,1:T(8,128)S(1)} %slice_add_fusion.4), channel_id=1, source_target_pairs={{1,0},{2,1},{3,2},{4,3},{5,4},{6,5},{7,6},{8,7},{9,8},{10,9},{11,1... | collective-permute-start | bytes 786440 | tf_op jit(solution)/shard_map/ppermute | solution.py:17
  175.8 7.7 %collective-permute-start.29 = (f32[128,512]{0,1:T(8,128)S(1)}, f32[128,512]{0,1:T(8,128)S(1)}, u32[]{:S(2)}, u32[]{:S(2)}) collective-permute-start(f32[128,512]{0,1:T(8,128)S(1)} %slice_add_fusion.11), channel_id=1, source_target_pairs={{1,0},{2,1},{3,2},{4,3},{5,4},{6,5},{7,6},{8,7},{9,8},{10,9},{11,1... | collective-permute-start | bytes 786440 | tf_op jit(solution)/shard_map/ppermute | solution.py:17
  177.2 8.6 %collective-permute-start.37 = (f32[128,512]{0,1:T(8,128)S(1)}, f32[128,512]{0,1:T(8,128)}, u32[]{:S(2)}, u32[]{:S(2)}) collective-permute-start(f32[128,512]{0,1:T(8,128)S(1)} %slice_add_fusion.3), channel_id=1, source_target_pairs={{1,0},{2,1},{3,2},{4,3},{5,4},{6,5},{7,6},{8,7},{9,8},{10,9},{11,1... | collective-permute-start | bytes 786440 | tf_op jit(solution)/shard_map/ppermute | solution.py:17
  184.5 8.1 %collective-permute-start.30 = (f32[128,512]{0,1:T(8,128)S(1)}, f32[128,512]{0,1:T(8,128)S(1)}, u32[]{:S(2)}, u32[]{:S(2)}) collective-permute-start(f32[128,512]{0,1:T(8,128)S(1)} %slice_add_fusion.10), channel_id=1, source_target_pairs={{1,0},{2,1},{3,2},{4,3},{5,4},{6,5},{7,6},{8,7},{9,8},{10,9},{11,1... | collective-permute-start | bytes 786440 | tf_op jit(solution)/shard_map/ppermute | solution.py:17
  186.8 8.7 %collective-permute-start.38 = (f32[128,512]{0,1:T(8,128)S(1)}, f32[128,512]{0,1:T(8,128)S(1)}, u32[]{:S(2)}, u32[]{:S(2)}) collective-permute-start(f32[128,512]{0,1:T(8,128)S(1)} %slice_add_fusion.2), channel_id=1, source_target_pairs={{1,0},{2,1},{3,2},{4,3},{5,4},{6,5},{7,6},{8,7},{9,8},{10,9},{11,1... | collective-permute-start | bytes 786440 | tf_op jit(solution)/shard_map/ppermute | solution.py:17
  193.6 68.9 %collective-permute-start.31 = (f32[128,512]{0,1:T(8,128)S(1)}, f32[128,512]{0,1:T(8,128)}, u32[]{:S(2)}, u32[]{:S(2)}) collective-permute-start(f32[128,512]{0,1:T(8,128)S(1)} %slice_add_fusion.9), channel_id=1, source_target_pairs={{1,0},{2,1},{3,2},{4,3},{5,4},{6,5},{7,6},{8,7},{9,8},{10,9},{11,1... | collective-permute-start | bytes 786440 | tf_op jit(solution)/shard_map/ppermute | solution.py:17
  195.5 68.8 %collective-permute-start.39 = (f32[128,512]{0,1:T(8,128)S(1)}, f32[128,512]{0,1:T(8,128)S(1)}, u32[]{:S(2)}, u32[]{:S(2)}) collective-permute-start(f32[128,512]{0,1:T(8,128)S(1)} %slice_add_fusion.1), channel_id=1, source_target_pairs={{1,0},{2,1},{3,2},{4,3},{5,4},{6,5},{7,6},{8,7},{9,8},{10,9},{11,1... | collective-permute-start | bytes 786440 | tf_op jit(solution)/shard_map/ppermute | solution.py:17
where the time goes:
time: 267 us; the launch traced here: 265 us
  starting transfers between devices  107 us (40%)
  blocking collectives  65 us (24%)
  local copies, waits for them, and re-layouts  27.1 us (10%)
  matrix products  25.9 us (10%)
  other arithmetic  23.4 us (9%)
  waiting for transfers between devices  14 us (5%)
    ppermute x40, starting transfers between devices, passed_along(): return lax.ppermute(block, axis, route)  107 us
    psum x1, blocking collectives, per_device(): sink_grad = lax.psum(sink_local, 'ctx')  65 us
    ppermute x40, waiting for transfers between devices, passed_along(): return lax.ppermute(block, axis, route)  14 us
    unnamed x79, local copies, waits for them, and re-layouts  13.7 us
    reshape x8, local copies, waits for them, and re-layouts, per_device(): query_list.append(query_part.reshape(tok_rows, groups * HEAD_DIM))  7.15 us
    add x7, other arithmetic, per_device(): moved[0] + block_of(key_partial, distance)  6.85 us
    dot_general x8, matrix products, group_grads(): jnp.einsum('gbl,ld->bgd', dscore, key_group, preferred_element_type=jnp.f...  5.96 us
    dot_general x8, matrix products, group_grads(): jnp.einsum('bgd,ld->gbl', grad_group, value_group, preferred_element_type...  5.56 us
  transfers between devices with their start and end apart: 40, of which 14 were waited for; matrix products, arithmetic and copies ran while one was open for 16% of the time, Pallas kernels for 0%

commit v1 on v0

v1 whole, which is shorter than its diff:
```python
import functools

import jax
import jax.numpy as jnp
from jax import lax
from jax.experimental import pallas as pl
from jax.experimental.pallas import tpu as pltpu
from jax.sharding import PartitionSpec as P

QUERY_HEADS = 32
KV_HEADS = 8
HEAD_DIM = 64
WINDOW = 1024
GROUPS = QUERY_HEADS // KV_HEADS
MESH = pl.DeviceIdType.MESH
F32 = jnp.float32
BF16 = jnp.bfloat16
MASKED = -1e30


def flip(index, mask):
    result = index
    for bit in (1, 2, 4):
        on = (mask // bit) % 2
        result = result + on * (bit - 2 * bit * ((index // bit) % 2))
    return result


def kernel(planes, chunk, sink_ref, q_ref, k_ref, v_ref, g_ref, seg_ref, oq_ref, ok_ref, ov_ref, os_ref,
           kvsend, segsend, kvbuf, segbuf, qbuf, gbuf, ktbuf, segcol, rhs, grhs, sd, ed, acc,
           qgs, kvgs, kvin, kvnx, sinkacc, sinkplanes, sinksum, sinkall,
           s_kv, r_kv, s_seg, r_seg, s_q, r_q, s_g, r_g, s_qg, r_qg, s_kg, r_kg, s_sa, r_sa, s_sb, r_sb):
    tok = q_ref.shape[0]
    side = KV_HEADS
    cols = GROUPS * HEAD_DIM
    lanes = GROUPS * tok
    span = WINDOW + tok
    me = lax.axis_index("ctx")
    l = me % side
    z = me // side
    base = z * side

    def rows(j):
        return pl.ds(pl.multiple_of(j * tok, tok), tok)

    def head_cols(d):
        return pl.ds(pl.multiple_of(d * cols, cols), cols)

    def remote(src, dst, ssem, rsem, device):
        return pltpu.make_async_remote_copy(
            src_ref=src, dst_ref=dst, send_sem=ssem, recv_sem=rsem,
            device_id=(device,), device_id_type=MESH)

    barrier = pltpu.get_barrier_semaphore()

    def greet(device):
        pl.semaphore_signal(barrier, inc=1, device_id=(device,), device_id_type=MESH)

    for k in range(1, side):
        greet(base + flip(l, k))

    @pl.when(z > 0)
    def _():
        for k in range(side):
            greet(base - side + k)

    @pl.when(z < planes - 1)
    def _():
        for k in range(side):
            greet(base + side + k)

    for p in range(planes):
        @pl.when((p > z + 1) | (p < z - 1))
        def _():
            greet(p * side + l)

    for h in range(side):
        part = slice(h * HEAD_DIM, (h + 1) * HEAD_DIM)
        kvsend[h] = jnp.concatenate([k_ref[:, part], v_ref[:, part]], 1)
    segsend[...] = jnp.broadcast_to(seg_ref[...].astype(F32), segsend.shape)
    kvbuf[rows(side + l), :] = kvsend[l]
    segbuf[side + l] = segsend[...]
    qbuf[l] = q_ref[:, head_cols(l)]
    gbuf[l] = g_ref[:, head_cols(l)]
    acc[...] = jnp.zeros_like(acc)
    sinkacc[...] = jnp.zeros_like(sinkacc)

    @pl.when(z == 0)
    def _():
        kvbuf[0:WINDOW, :] = jnp.zeros((WINDOW, kvbuf.shape[1]), BF16)
        segbuf[0:side] = jnp.full((side,) + segbuf.shape[1:], -1.0, F32)

    @pl.when(z == planes - 1)
    def _():
        kvnx[...] = jnp.zeros_like(kvnx)

    ends = (z + planes - 1) // planes + (2 * planes - 2 - z) // planes
    pl.semaphore_wait(barrier, side - 1 + planes - 1 + (side - 1) * ends)

    def kv_next(k):
        d = flip(l, k)
        return (remote(kvsend.at[d], kvbuf.at[rows(l)], s_kv.at[k], r_kv.at[l], base + side + d),
                remote(segsend, segbuf.at[l], s_seg.at[k], r_seg.at[l], base + side + d))

    def kv_own(k):
        d = flip(l, k)
        return (remote(kvsend.at[d], kvbuf.at[rows(side + l)], s_kv.at[side + k], r_kv.at[side + l], base + d),
                remote(segsend, segbuf.at[side + l], s_seg.at[side + k], r_seg.at[side + l], base + d))

    def qg_to(k):
        d = flip(l, k)
        return (remote(q_ref.at[:, head_cols(d)], qbuf.at[l], s_q.at[k], r_q.at[l], base + d),
                remote(g_ref.at[:, head_cols(d)], gbuf.at[l], s_g.at[k], r_g.at[l], base + d))

    @pl.when(z < planes - 1)
    def _():
        for k in range(side):
            for copy in kv_next(k):
                copy.start()

    for k in range(1, side):
        for copy in kv_own(k):
            copy.start()
    for k in range(1, side):
        for copy in qg_to(k):
            copy.start()

    other = base + flip(l, 1)

    def kv_arrive(j):
        remote(kvsend.at[0], kvbuf.at[rows(j)], s_kv.at[0], r_kv.at[j], other).wait_recv()
        remote(segsend, segbuf.at[j], s_seg.at[0], r_seg.at[j], other).wait_recv()

    for k in range(1, side):
        kv_arrive(side + flip(l, k))

    @pl.when(z > 0)
    def _():
        for k in range(side):
            kv_arrive(k)

    for j in range(2 * side):
        block = kvbuf[j * tok:(j + 1) * tok, :].astype(F32)
        ktbuf[:, j * tok:(j + 1) * tok] = block.T[:HEAD_DIM].astype(BF16)
        segcol[j * tok:(j + 1) * tok, :] = jnp.broadcast_to(segbuf[j, 0:1], (tok, tok)).T

    sink_row = jnp.concatenate(
        [jnp.full((1, tok), sink_ref[GROUPS * l + h], F32) for h in range(GROUPS)], 1)
    zero = jnp.zeros((tok, HEAD_DIM), BF16)

    def qg_back(k):
        b = flip(l, k)
        return remote(qgs.at[b], oq_ref.at[:, head_cols(l)], s_qg.at[b], r_qg.at[l], base + b)

    def step(k, carry):
        b = flip(l, k)

        @pl.when(k > 0)
        def _():
            remote(q_ref.at[:, head_cols(0)], qbuf.at[b], s_q.at[0], r_q.at[b], other).wait_recv()
            remote(g_ref.at[:, head_cols(0)], gbuf.at[b], s_g.at[0], r_g.at[b], other).wait_recv()

        q = (qbuf[b].astype(F32) * 0.125).astype(BF16)
        g = gbuf[b]
        for h in range(GROUPS):
            part = slice(h * HEAD_DIM, (h + 1) * HEAD_DIM)
            rhs[h * tok:(h + 1) * tok, :] = jnp.concatenate([q[:, part], zero], 1)
            rhs[lanes + h * tok:lanes + (h + 1) * tok, :] = jnp.concatenate([zero, g[:, part]], 1)

        seg_row = segbuf[side + b, 0:1, :]
        start = pl.multiple_of(b * tok, tok)
        lane = lax.broadcasted_iota(jnp.int32, (chunk, tok), 1)
        sub = lax.broadcasted_iota(jnp.int32, (chunk, tok), 0)

        def scores(c, top):
            first = pl.multiple_of(c * chunk, chunk)
            both = lax.dot_general(kvbuf[pl.ds(start + first, chunk), :], rhs[...],
                                   (((1,), (1,)), ((), ())), preferred_element_type=F32)
            rel = sub + first - lane
            keep = (rel > 0) & (rel <= WINDOW) & (segcol[pl.ds(start + first, chunk), :] == seg_row)
            tops = []
            for h in range(GROUPS):
                part = jnp.where(keep, both[:, h * tok:(h + 1) * tok], MASKED)
                sd[pl.ds(first, chunk), h * tok:(h + 1) * tok] = part
                tops.append(jnp.max(part.reshape(chunk // 8, 8, tok), 0))
            sd[pl.ds(first, chunk), lanes:] = both[:, lanes:]
            return jnp.maximum(top, jnp.concatenate(tops, 1))

        top = lax.fori_loop(0, span // chunk, scores, jnp.broadcast_to(sink_row, (8, lanes)))
        top = jnp.max(top, 0, keepdims=True)

        small = chunk // 3

        def expd(c, carry):
            total, mixed = carry
            first = pl.multiple_of(c * small, small)
            e = jnp.exp(sd[pl.ds(first, small), :lanes] - top)
            dp = sd[pl.ds(first, small), lanes:]
            sd[pl.ds(first, small), :lanes] = e
            ed[pl.ds(first, small), lanes:] = e.astype(BF16)
            total = total + jnp.sum(e.reshape(small // 8, 8, lanes), 0)
            mixed = mixed + jnp.sum((e * dp).reshape(small // 8, 8, lanes), 0)
            return total, mixed

        empty = jnp.zeros((8, lanes), F32)
        total, mixed = lax.fori_loop(0, span // small, expd, (empty, empty))
        sink_exp = jnp.exp(sink_row - top)
        inv = 1.0 / (jnp.sum(total, 0, keepdims=True) + sink_exp)
        delta = jnp.sum(mixed, 0, keepdims=True) * inv
        sinkacc[...] = sinkacc[...] - jnp.broadcast_to(sink_exp * inv * delta, sinkacc.shape)

        for h in range(GROUPS):
            inv_col = jnp.broadcast_to(inv[:, h * tok:(h + 1) * tok], (tok, tok)).T
            for r in (h * tok, lanes + h * tok):
                grhs[r:r + tok, :] = (rhs[r:r + tok, :].astype(F32) * inv_col).astype(BF16)

        def grads(c, qgt):
            first = pl.multiple_of(c * chunk, chunk)
            d = (sd[pl.ds(first, chunk), :lanes] * (sd[pl.ds(first, chunk), lanes:] - delta)).astype(BF16)
            ed[pl.ds(first, chunk), :lanes] = d
            acc[pl.ds(start + first, chunk), :] += jnp.dot(
                ed[pl.ds(first, chunk), :], grhs[...], preferred_element_type=F32)
            return qgt + jnp.dot(ktbuf[:, pl.ds(pl.multiple_of(start + first, tok), chunk)], d,
                                 preferred_element_type=F32)

        qgt = lax.fori_loop(0, span // chunk, grads, jnp.zeros((HEAD_DIM, lanes), F32))
        qgt = qgt * (inv * 0.125)
        for pair in range(GROUPS // 2):
            two = jnp.concatenate(
                [qgt[:, (2 * pair + i) * tok:(2 * pair + i + 1) * tok] for i in (0, 1)], 0)
            qgs[b, :, pair * tok:(pair + 1) * tok] = two.T.astype(BF16)

        @pl.when(k > 0)
        def _():
            qg_back(k).start()
        return carry

    lax.fori_loop(0, side, step, 0)

    for j in range(2 * side):
        kvgs[j] = acc[j * tok:(j + 1) * tok, :].astype(BF16)
    for h in range(GROUPS):
        sinksum[h:h + 1, :] = sinkacc[0:1, h * tok:(h + 1) * tok]
    sinksum[GROUPS:, :] = jnp.zeros((8 - GROUPS, tok), F32)
    oq_ref[:, head_cols(l)] = qgs[l]
    kvin[l] = kvgs[side + l]
    sinkplanes[z] = sinksum[...]

    def kg_prev(k):
        d = flip(l, k)
        return remote(kvgs.at[d], kvnx.at[l], s_kg.at[k], r_kg.at[l], base - side + d)

    def kg_own(k):
        d = flip(l, k)
        return remote(kvgs.at[side + d], kvin.at[l], s_kg.at[side + k], r_kg.at[side + l], base + d)

    def sink_to(p):
        return remote(sinksum, sinkplanes.at[z], s_sa.at[p], r_sa.at[z], p * side + l)

    @pl.when(z > 0)
    def _():
        for k in range(side):
            kg_prev(k).start()

    for p in range(planes):
        @pl.when(p != z)
        def _():
            sink_to(p).start()

    for k in range(1, side):
        kg_own(k).start()

    for p in range(planes):
        @pl.when(p != z)
        def _():
            remote(sinksum, sinkplanes.at[p], s_sa.at[p], r_sa.at[p], other).wait_recv()

    sinkall[l] = jnp.sum(sinkplanes[...], 0)

    def sink_side(k):
        return remote(sinkall.at[l], sinkall.at[l], s_sb.at[k], r_sb.at[l], base + flip(l, k))

    for k in range(1, side):
        sink_side(k).start()

    for k in range(1, side):
        j = flip(l, k)
        remote(kvgs.at[0], kvin.at[j], s_kg.at[0], r_kg.at[side + j], other).wait_recv()

    @pl.when(z < planes - 1)
    def _():
        for k in range(side):
            remote(kvgs.at[0], kvnx.at[k], s_kg.at[0], r_kg.at[k], other).wait_recv()

    for pair in range(side // 2):
        two = [kvin[2 * pair + i].astype(F32) + kvnx[2 * pair + i].astype(F32) for i in (0, 1)]
        part = slice(pair * 2 * HEAD_DIM, (pair + 1) * 2 * HEAD_DIM)
        ok_ref[:, part] = jnp.concatenate([t[:, :HEAD_DIM] for t in two], 1).astype(BF16)
        ov_ref[:, part] = jnp.concatenate([t[:, HEAD_DIM:] for t in two], 1).astype(BF16)

    for k in range(1, side):
        j = flip(l, k)
        remote(sinkall.at[j], sinkall.at[j], s_sb.at[0], r_sb.at[j], other).wait_recv()
    os_ref[...] = jnp.sum(sinkall[...], -1)

    for k in range(1, side):
        j = flip(l, k)
        remote(qgs.at[0], oq_ref.at[:, head_cols(j)], s_qg.at[0], r_qg.at[j], other).wait_recv()

    @pl.when(z < planes - 1)
    def _():
        for k in range(side):
            for copy in kv_next(k):
                copy.wait_send()

    @pl.when(z > 0)
    def _():
        for k in range(side):
            kg_prev(k).wait_send()

    for p in range(planes):
        @pl.when(p != z)
        def _():
            sink_to(p).wait_send()

    for k in range(1, side):
        for copy in kv_own(k) + qg_to(k) + (qg_back(k), kg_own(k), sink_side(k)):
            copy.wait_send()


def per_device(queries, key_heads, value_heads, out_grad, segment, sink_logits):
    tok = queries.shape[0]
    planes = lax.axis_size("ctx") // KV_HEADS
    side = KV_HEADS
    cols = GROUPS * HEAD_DIM
    lanes = GROUPS * tok
    span = WINDOW + tok
    chunk = span // 3
    wide = 2 * HEAD_DIM
    vmem = pl.BlockSpec(memory_space=pltpu.VMEM)
    dma = pltpu.SemaphoreType.DMA
    scratch = [
        pltpu.VMEM((side, tok, wide), BF16),
        pltpu.VMEM((8, tok), F32),
        pltpu.VMEM((2 * WINDOW, wide), BF16),
        pltpu.VMEM((2 * side, 8, tok), F32),
        pltpu.VMEM((side, tok, cols), BF16),
        pltpu.VMEM((side, tok, cols), BF16),
        pltpu.VMEM((HEAD_DIM, 2 * WINDOW), BF16),
        pltpu.VMEM((2 * WINDOW, tok), F32),
        pltpu.VMEM((2 * lanes, wide), BF16),
        pltpu.VMEM((2 * lanes, wide), BF16),
        pltpu.VMEM((span, 2 * lanes), F32),
        pltpu.VMEM((span, 2 * lanes), BF16),
        pltpu.VMEM((2 * WINDOW, wide), F32),
        pltpu.VMEM((side, tok, cols), BF16),
        pltpu.VMEM((2 * side, tok, wide), BF16),
        pltpu.VMEM((side, tok, wide), BF16),
        pltpu.VMEM((side, tok, wide), BF16),
        pltpu.VMEM((8, lanes), F32),
        pltpu.VMEM((planes, 8, tok), F32),
        pltpu.VMEM((8, tok), F32),
        pltpu.VMEM((side, 8, tok), F32),
        dma((2 * side,)), dma((2 * side,)), dma((2 * side,)), dma((2 * side,)),
        dma((side,)), dma((side,)), dma((side,)), dma((side,)),
        dma((side,)), dma((side,)), dma((2 * side,)), dma((2 * side,)),
        dma((planes,)), dma((planes,)), dma((side,)), dma((side,)),
    ]
    query_grad, key_grad, value_grad, sink = pl.pallas_call(
        functools.partial(kernel, planes, chunk),
        out_shape=(
            jax.ShapeDtypeStruct(queries.shape, BF16),
            jax.ShapeDtypeStruct(key_heads.shape, BF16),
            jax.ShapeDtypeStruct(value_heads.shape, BF16),
            jax.ShapeDtypeStruct((side, 8), F32),
        ),
        in_specs=[pl.BlockSpec(memory_space=pltpu.SMEM)] + [vmem] * 5,
        out_specs=(vmem,) * 4,
        scratch_shapes=scratch,
        compiler_params=pltpu.CompilerParams(
            collective_id=0, has_side_effects=True, vmem_limit_bytes=48 * 1024 * 1024),
    )(sink_logits, queries, key_heads, value_heads, out_grad, segment.reshape(1, tok))
    return query_grad, key_grad, value_grad, sink[:, :GROUPS].reshape(-1)


def solution(mesh):
    return jax.shard_map(
        per_device,
        mesh=mesh,
        in_specs=(P("ctx", None), P("ctx", None), P("ctx", None), P("ctx", None), P("ctx"), P()),
        out_specs=(P("ctx", None), P("ctx", None), P("ctx", None), P()),
        check_vma=False,
    )
```

time: 267 us -> 64.6 us (0.24)
  starting transfers between devices: 107 us -> 0 us
  blocking collectives: 65 us -> 0 us
  Pallas kernels: 0 us -> 56.5 us
  matrix products: 25.9 us -> 0 us
  other arithmetic: 23.4 us -> 0 us
  local copies, waits for them, and re-layouts: 27.1 us -> 7.24 us
  waiting for transfers between devices: 14 us -> 0 us
    ppermute x40 -> x0, starting transfers between devices: 107 us -> none  [passed_along(): return lax.ppermute(block, axis, route)]
    psum x1 -> x0, blocking collectives: 65 us -> none  [per_device(): sink_grad = lax.psum(sink_local, 'ctx')]
    pallas_call x0 -> x1, Pallas kernels: none -> 56.5 us  [per_device(): pl.pallas_call(functools.partial(kernel, planes, chunk), out_shape=(jax.S...]
    dot_general x40 -> x0, matrix products: 23.2 us -> none  [the longest x8 5.96 us: group_grads(): jnp.einsum('gbl,ld->bgd', dscore, key_group, preferred_element_type=jnp.f...]
    ppermute x40 -> x0, waiting for transfers between devices: 14 us -> none  [passed_along(): return lax.ppermute(block, axis, route)]
    add x24 -> x0, other arithmetic: 9.96 us -> none  [the longest x7 6.85 us: per_device(): moved[0] + block_of(key_partial, distance)]
    unnamed x79 -> x15, local copies, waits for them, and re-layouts: 13.7 us -> 6.65 us
    reshape x8 -> x1, local copies, waits for them, and re-layouts: 7.15 us -> 0.59 us  [per_device(): return (query_grad, key_grad, value_grad, sink[:, :GROUPS].reshape(-1))]
  transfers between devices with their start and end apart: 40 -> 0, of which waited for: 14 -> 0; matrix products, arithmetic and copies ran while one was open for 16% -> 0% of each run, Pallas kernels for 0% -> 0%
where the time goes in v1:
time: 64.6 us; the launch traced here: 64.4 us
  Pallas kernels  56.5 us (87%)
  local copies, waits for them, and re-layouts  7.24 us (11%)
  between operations  0.66 us (1%)
    pallas_call x1, Pallas kernels, per_device(): pl.pallas_call(functools.partial(kernel, planes, chunk), out_shape=(jax.S...  56.5 us
    unnamed x15, local copies, waits for them, and re-layouts  6.65 us

profile of v1, /device:TPU:0, one launch (start us, length us, event | category | flops | bytes accessed | tf_op | source)
XLA Modules:
  0.0 64.4 jit_solution(11717408193073704722)
XLA Ops:
  0.6 0.0 copy-start.4
  0.6 0.0 copy-start.5
  0.7 0.6 copy-done.4
  1.3 0.0 copy-done.5
  1.3 0.0 copy-start
  1.3 1.0 %copy-done = bf16[128,2048]{1,0:T(8,128)(2,1)S(1)} copy-done((bf16[128,2048]{1,0:T(8,128)(2,1)S(1)}, bf16[128,2048]{1,0:T(8,128)(2,1)}, u32[]{:S(2)}) %copy-start) | copy-done | bytes 524312
  2.3 0.0 copy-start.1
  2.3 1.0 %copy-done.1 = bf16[128,2048]{1,0:T(8,128)(2,1)S(1)} copy-done((bf16[128,2048]{1,0:T(8,128)(2,1)S(1)}, bf16[128,2048]{1,0:T(8,128)(2,1)}, u32[]{:S(2)}) %copy-start.1) | copy-done | bytes 524312
  3.4 0.0 copy-start.2
  3.4 0.9 %copy-done.2 = bf16[128,512]{1,0:T(8,128)(2,1)S(1)} copy-done((bf16[128,512]{1,0:T(8,128)(2,1)S(1)}, bf16[128,512]{1,0:T(8,128)(2,1)}, u32[]{:S(2)}) %copy-start.2) | copy-done | bytes 131096
  4.3 0.0 copy-start.3
  4.3 0.9 %copy-done.3 = bf16[128,512]{1,0:T(8,128)(2,1)S(1)} copy-done((bf16[128,512]{1,0:T(8,128)(2,1)S(1)}, bf16[128,512]{1,0:T(8,128)(2,1)}, u32[]{:S(2)}) %copy-start.3) | copy-done | bytes 131096
  5.2 56.5 %shard_map.93 = (bf16[128,2048]{1,0:T(8,128)(2,1)S(1)}, bf16[128,512]{1,0:T(8,128)(2,1)S(1)}, bf16[128,512]{1,0:T(8,128)(2,1)S(1)}, f32[8,8]{1,0:T(8,128)S(1)}) custom-call(f32[32]{0:T(128)S(1)} %copy-done.4, bf16[128,2048]{1,0:T(8,128)(2,1)S(1)} %copy-done, bf16[128,512]{1,0:T(8,128)(2,1)S(1)} %copy-done.2, bf16[128,512]{1,0:T(8,128)(2,1)S(1)} %copy-done.3, ...), custom_call_target="tpu_custom_call" | custom-call | tf_op jit(solution)/shard_map/pallas_call | solution.py:369
  61.7 0.6 reshape.15
  62.3 0.8 %copy.13 = bf16[128,2048]{1,0:T(8,128)(2,1)} copy(bf16[128,2048]{1,0:T(8,128)(2,1)S(1)} %get-tuple-element.16) | data formatting | bytes 1048576
  63.1 0.7 %copy.14 = bf16[128,512]{1,0:T(8,128)(2,1)} copy(bf16[128,512]{1,0:T(8,128)(2,1)S(1)} %get-tuple-element.17) | data formatting | bytes 262144
  63.7 0.7 %copy.15 = bf16[128,512]{1,0:T(8,128)(2,1)} copy(bf16[128,512]{1,0:T(8,128)(2,1)S(1)} %get-tuple-element.18) | data formatting | bytes 262144
Async XLA Ops:
  0.6 0.7 %copy-start.4 = (f32[32]{0:T(128)S(1)}, f32[32]{0:T(128)}, u32[]{:S(2)}) copy-start(f32[32]{0:T(128)} %sink_ref.1) | copy-start | bytes 388
  0.6 0.7 %copy-start.5 = (s32[128]{0:T(128)S(1)}, s32[128]{0:T(128)}, u32[]{:S(2)}) copy-start(s32[128]{0:T(128)} %param.10) | copy-start | bytes 1540
  1.3 1.0 %copy-start = (bf16[128,2048]{1,0:T(8,128)(2,1)S(1)}, bf16[128,2048]{1,0:T(8,128)(2,1)}, u32[]{:S(2)}) copy-start(bf16[128,2048]{1,0:T(8,128)(2,1)} %q_ref.1) | copy-start | bytes 1572868
  2.3 1.0 %copy-start.1 = (bf16[128,2048]{1,0:T(8,128)(2,1)S(1)}, bf16[128,2048]{1,0:T(8,128)(2,1)}, u32[]{:S(2)}) copy-start(bf16[128,2048]{1,0:T(8,128)(2,1)} %g_ref.1) | copy-start | bytes 1572868
  3.4 0.9 %copy-start.2 = (bf16[128,512]{1,0:T(8,128)(2,1)S(1)}, bf16[128,512]{1,0:T(8,128)(2,1)}, u32[]{:S(2)}) copy-start(bf16[128,512]{1,0:T(8,128)(2,1)} %k_ref.1) | copy-start | bytes 393220
  4.3 0.9 %copy-start.3 = (bf16[128,512]{1,0:T(8,128)(2,1)S(1)}, bf16[128,512]{1,0:T(8,128)(2,1)}, u32[]{:S(2)}) copy-start(bf16[128,512]{1,0:T(8,128)(2,1)} %v_ref.1) | copy-start | bytes 393220

commit v2 on v1

--- a/solution.py
+++ b/solution.py
@@ -26,8 +26,8 @@
     return result
 
 
-def kernel(planes, chunk, sink_ref, q_ref, k_ref, v_ref, g_ref, seg_ref, oq_ref, ok_ref, ov_ref, os_ref,
-           kvsend, segsend, kvbuf, segbuf, qbuf, gbuf, ktbuf, segcol, rhs, grhs, sd, ed, acc,
+def kernel(planes, chunk, sink_hbm, q_ref, k_hbm, v_hbm, g_ref, seg_hbm, oq_ref, ok_ref, ov_ref, os_ref,
+           sink_ref, k_ref, v_ref, seg_ref, s_in, kvsend, segsend, kvbuf, segbuf, qbuf, gbuf, ktbuf, segcol, rhs, grhs, sd, ed, acc,
            qgs, kvgs, kvin, kvnx, sinkacc, sinkplanes, sinksum, sinkall,
            s_kv, r_kv, s_seg, r_seg, s_q, r_q, s_g, r_g, s_qg, r_qg, s_kg, r_kg, s_sa, r_sa, s_sb, r_sb):
     tok = q_ref.shape[0]
@@ -51,6 +51,17 @@
             src_ref=src, dst_ref=dst, send_sem=ssem, recv_sem=rsem,
             device_id=(device,), device_id_type=MESH)
 
+    inputs = [
+        pltpu.make_async_copy(k_hbm, k_ref, s_in.at[0]),
+        pltpu.make_async_copy(v_hbm, v_ref, s_in.at[1]),
+        pltpu.make_async_copy(seg_hbm, seg_ref, s_in.at[2]),
+        pltpu.make_async_copy(sink_hbm, sink_ref, s_in.at[3]),
+        pltpu.make_async_copy(q_ref.at[:, head_cols(l)], qbuf.at[l], s_in.at[4]),
+        pltpu.make_async_copy(g_ref.at[:, head_cols(l)], gbuf.at[l], s_in.at[5]),
+    ]
+    for copy in inputs:
+        copy.start()
+
     barrier = pltpu.get_barrier_semaphore()
 
     def greet(device):
@@ -74,14 +85,14 @@
         def _():
             greet(p * side + l)
 
+    for copy in inputs[:3]:
+        copy.wait()
     for h in range(side):
         part = slice(h * HEAD_DIM, (h + 1) * HEAD_DIM)
         kvsend[h] = jnp.concatenate([k_ref[:, part], v_ref[:, part]], 1)
     segsend[...] = jnp.broadcast_to(seg_ref[...].astype(F32), segsend.shape)
     kvbuf[rows(side + l), :] = kvsend[l]
     segbuf[side + l] = segsend[...]
-    qbuf[l] = q_ref[:, head_cols(l)]
-    gbuf[l] = g_ref[:, head_cols(l)]
     acc[...] = jnp.zeros_like(acc)
     sinkacc[...] = jnp.zeros_like(sinkacc)
 
@@ -144,6 +155,8 @@
         ktbuf[:, j * tok:(j + 1) * tok] = block.T[:HEAD_DIM].astype(BF16)
         segcol[j * tok:(j + 1) * tok, :] = jnp.broadcast_to(segbuf[j, 0:1], (tok, tok)).T
 
+    for copy in inputs[3:]:
+        copy.wait()
     sink_row = jnp.concatenate(
         [jnp.full((1, tok), sink_ref[GROUPS * l + h], F32) for h in range(GROUPS)], 1)
     zero = jnp.zeros((tok, HEAD_DIM), BF16)
@@ -152,58 +165,72 @@
         b = flip(l, k)
         return remote(qgs.at[b], oq_ref.at[:, head_cols(l)], s_qg.at[b], r_qg.at[l], base + b)
 
-    def step(k, carry):
+    lane = lax.broadcasted_iota(jnp.int32, (chunk, tok), 1)
+    sub = lax.broadcasted_iota(jnp.int32, (chunk, tok), 0)
+    floor = jnp.broadcast_to(sink_row, (8, lanes))
+    empty = jnp.zeros((8, lanes), F32)
+
+    def prepare(k, slot):
         b = flip(l, k)
-
-        @pl.when(k > 0)
-        def _():
-            remote(q_ref.at[:, head_cols(0)], qbuf.at[b], s_q.at[0], r_q.at[b], other).wait_recv()
-            remote(g_ref.at[:, head_cols(0)], gbuf.at[b], s_g.at[0], r_g.at[b], other).wait_recv()
-
         q = (qbuf[b].astype(F32) * 0.125).astype(BF16)
         g = gbuf[b]
         for h in range(GROUPS):
             part = slice(h * HEAD_DIM, (h + 1) * HEAD_DIM)
-            rhs[h * tok:(h + 1) * tok, :] = jnp.concatenate([q[:, part], zero], 1)
-            rhs[lanes + h * tok:lanes + (h + 1) * tok, :] = jnp.concatenate([zero, g[:, part]], 1)
-
+            rhs[slot, h * tok:(h + 1) * tok, :] = jnp.concatenate([q[:, part], zero], 1)
+            rhs[slot, lanes + h * tok:lanes + (h + 1) * tok, :] = jnp.concatenate([zero, g[:, part]], 1)
+
+    def arrive(k):
+        b = flip(l, k)
+        remote(q_ref.at[:, head_cols(0)], qbuf.at[b], s_q.at[0], r_q.at[b], other).wait_recv()
+        remote(g_ref.at[:, head_cols(0)], gbuf.at[b], s_g.at[0], r_g.at[b], other).wait_recv()
+
+    def scores(c, k, slot, top):
+        b = flip(l, k)
         seg_row = segbuf[side + b, 0:1, :]
+        first = pl.multiple_of(c * chunk, chunk)
+        at = pl.ds(pl.multiple_of(b * tok + c * chunk, tok), chunk)
+        both = lax.dot_general(kvbuf[at, :], rhs[slot],
+                               (((1,), (1,)), ((), ())), preferred_element_type=F32)
+        rel = sub + first - lane
+        keep = (rel > 0) & (rel <= WINDOW) & (segcol[at, :] == seg_row)
+        tops = []
+        for h in range(GROUPS):
+            part = jnp.where(keep, both[:, h * tok:(h + 1) * tok], MASKED)
+            sd[slot, pl.ds(first, chunk), h * tok:(h + 1) * tok] = part
+            tops.append(jnp.max(part.reshape(chunk // 8, 8, tok), 0))
+        sd[slot, pl.ds(first, chunk), lanes:] = both[:, lanes:]
+        return jnp.maximum(top, jnp.concatenate(tops, 1))
+
+    def expd(c, slot, top, total, mixed):
+        first = pl.multiple_of(c * chunk, chunk)
+        e = jnp.exp(sd[slot, pl.ds(first, chunk), :lanes] - top)
+        dp = sd[slot, pl.ds(first, chunk), lanes:]
+        sd[slot, pl.ds(first, chunk), :lanes] = e
+        ed[pl.ds(first, chunk), lanes:] = e.astype(BF16)
+        total = total + jnp.sum(e.reshape(chunk // 8, 8, lanes), 0)
+        mixed = mixed + jnp.sum((e * dp).reshape(chunk // 8, 8, lanes), 0)
+        return total, mixed
+
+    def step(k, top, last):
+        b = flip(l, k)
+        slot = k % 2
         start = pl.multiple_of(b * tok, tok)
-        lane = lax.broadcasted_iota(jnp.int32, (chunk, tok), 1)
-        sub = lax.broadcasted_iota(jnp.int32, (chunk, tok), 0)
-
-        def scores(c, top):
-            first = pl.multiple_of(c * chunk, chunk)
-            both = lax.dot_general(kvbuf[pl.ds(start + first, chunk), :], rhs[...],
-                                   (((1,), (1,)), ((), ())), preferred_element_type=F32)
-            rel = sub + first - lane
-            keep = (rel > 0) & (rel <= WINDOW) & (segcol[pl.ds(start + first, chunk), :] == seg_row)
-            tops = []
-            for h in range(GROUPS):
-                part = jnp.where(keep, both[:, h * tok:(h + 1) * tok], MASKED)
-                sd[pl.ds(first, chunk), h * tok:(h + 1) * tok] = part
-                tops.append(jnp.max(part.reshape(chunk // 8, 8, tok), 0))
-            sd[pl.ds(first, chunk), lanes:] = both[:, lanes:]
-            return jnp.maximum(top, jnp.concatenate(tops, 1))
-
-        top = lax.fori_loop(0, span // chunk, scores, jnp.broadcast_to(sink_row, (8, lanes)))
         top = jnp.max(top, 0, keepdims=True)
 
-        small = chunk // 3
-
-        def expd(c, carry):
-            total, mixed = carry
-            first = pl.multiple_of(c * small, small)
-            e = jnp.exp(sd[pl.ds(first, small), :lanes] - top)
-            dp = sd[pl.ds(first, small), lanes:]
-            sd[pl.ds(first, small), :lanes] = e
-            ed[pl.ds(first, small), lanes:] = e.astype(BF16)
-            total = total + jnp.sum(e.reshape(small // 8, 8, lanes), 0)
-            mixed = mixed + jnp.sum((e * dp).reshape(small // 8, 8, lanes), 0)
-            return total, mixed
-
-        empty = jnp.zeros((8, lanes), F32)
-        total, mixed = lax.fori_loop(0, span // small, expd, (empty, empty))
+        if last:
+            ahead = floor
+            total, mixed = lax.fori_loop(0, span // chunk, lambda c, t: expd(c, slot, top, *t), (empty, empty))
+        else:
+            arrive(k + 1)
+            prepare(k + 1, 1 - slot)
+
+            def both(c, carry):
+                ahead, total, mixed = carry
+                ahead = scores(c, k + 1, 1 - slot, ahead)
+                return (ahead,) + expd(c, slot, top, total, mixed)
+
+            ahead, total, mixed = lax.fori_loop(0, span // chunk, both, (floor, empty, empty))
+
         sink_exp = jnp.exp(sink_row - top)
         inv = 1.0 / (jnp.sum(total, 0, keepdims=True) + sink_exp)
         delta = jnp.sum(mixed, 0, keepdims=True) * inv
@@ -212,11 +239,12 @@
         for h in range(GROUPS):
             inv_col = jnp.broadcast_to(inv[:, h * tok:(h + 1) * tok], (tok, tok)).T
             for r in (h * tok, lanes + h * tok):
-                grhs[r:r + tok, :] = (rhs[r:r + tok, :].astype(F32) * inv_col).astype(BF16)
+                grhs[r:r + tok, :] = (rhs[slot, r:r + tok, :].astype(F32) * inv_col).astype(BF16)
 
         def grads(c, qgt):
             first = pl.multiple_of(c * chunk, chunk)
-            d = (sd[pl.ds(first, chunk), :lanes] * (sd[pl.ds(first, chunk), lanes:] - delta)).astype(BF16)
+            d = (sd[slot, pl.ds(first, chunk), :lanes]
+                 * (sd[slot, pl.ds(first, chunk), lanes:] - delta)).astype(BF16)
             ed[pl.ds(first, chunk), :lanes] = d
             acc[pl.ds(start + first, chunk), :] += jnp.dot(
                 ed[pl.ds(first, chunk), :], grhs[...], preferred_element_type=F32)
@@ -233,9 +261,12 @@
         @pl.when(k > 0)
         def _():
             qg_back(k).start()
-        return carry
-
-    lax.fori_loop(0, side, step, 0)
+        return ahead
+
+    prepare(0, 0)
+    top = lax.fori_loop(0, span // chunk, lambda c, t: scores(c, 0, 0, t), floor)
+    top = lax.fori_loop(0, side - 1, lambda k, t: step(k, t, False), top)
+    step(side - 1, top, True)
 
     for j in range(2 * side):
         kvgs[j] = acc[j * tok:(j + 1) * tok, :].astype(BF16)
@@ -301,7 +332,13 @@
     for k in range(1, side):
         j = flip(l, k)
         remote(sinkall.at[j], sinkall.at[j], s_sb.at[0], r_sb.at[j], other).wait_recv()
-    os_ref[...] = jnp.sum(sinkall[...], -1)
+    place = lax.broadcasted_iota(jnp.int32, sinkall.shape, 2)
+    spot = (lax.broadcasted_iota(jnp.int32, sinkall.shape, 0) * GROUPS
+            + lax.broadcasted_iota(jnp.int32, sinkall.shape, 1))
+    head = lax.broadcasted_iota(jnp.int32, sinkall.shape, 1)
+    sums = jnp.sum(sinkall[...], -1, keepdims=True)
+    sums = jnp.sum(jnp.where((place == spot) & (head < GROUPS), sums, 0.0), 0)
+    os_ref[...] = jnp.sum(sums, 0, keepdims=True)[:, :QUERY_HEADS]
 
     for k in range(1, side):
         j = flip(l, k)
@@ -326,6 +363,14 @@
     for k in range(1, side):
         for copy in kv_own(k) + qg_to(k) + (qg_back(k), kg_own(k), sink_side(k)):
             copy.wait_send()
+
+
+def write_out(*refs):
+    copies = [pltpu.make_async_copy(refs[i], refs[4 + i], refs[8].at[i]) for i in range(4)]
+    for copy in copies:
+        copy.start()
+    for copy in copies:
+        copy.wait()
 
 
 def per_device(queries, key_heads, value_heads, out_grad, segment, sink_logits):
@@ -339,7 +384,13 @@
     wide = 2 * HEAD_DIM
     vmem = pl.BlockSpec(memory_space=pltpu.VMEM)
     dma = pltpu.SemaphoreType.DMA
+    hbm = pl.BlockSpec(memory_space=pltpu.HBM)
     scratch = [
+        pltpu.SMEM((QUERY_HEADS,), F32),
+        pltpu.VMEM(key_heads.shape, BF16),
+        pltpu.VMEM(key_heads.shape, BF16),
+        pltpu.VMEM((1, tok), jnp.int32),
+        dma((6,)),
         pltpu.VMEM((side, tok, wide), BF16),
         pltpu.VMEM((8, tok), F32),
         pltpu.VMEM((2 * WINDOW, wide), BF16),
@@ -348,9 +399,9 @@
         pltpu.VMEM((side, tok, cols), BF16),
         pltpu.VMEM((HEAD_DIM, 2 * WINDOW), BF16),
         pltpu.VMEM((2 * WINDOW, tok), F32),
+        pltpu.VMEM((2, 2 * lanes, wide), BF16),
         pltpu.VMEM((2 * lanes, wide), BF16),
-        pltpu.VMEM((2 * lanes, wide), BF16),
-        pltpu.VMEM((span, 2 * lanes), F32),
+        pltpu.VMEM((2, span, 2 * lanes), F32),
         pltpu.VMEM((span, 2 * lanes), BF16),
         pltpu.VMEM((2 * WINDOW, wide), F32),
         pltpu.VMEM((side, tok, cols), BF16),
@@ -366,21 +417,30 @@
         dma((side,)), dma((side,)), dma((2 * side,)), dma((2 * side,)),
         dma((planes,)), dma((planes,)), dma((side,)), dma((side,)),
     ]
-    query_grad, key_grad, value_grad, sink = pl.pallas_call(
+    shapes = (
+        jax.ShapeDtypeStruct(queries.shape, BF16),
+        jax.ShapeDtypeStruct(key_heads.shape, BF16),
+        jax.ShapeDtypeStruct(value_heads.shape, BF16),
+        jax.ShapeDtypeStruct((1, QUERY_HEADS), F32),
+    )
+    results = pl.pallas_call(
         functools.partial(kernel, planes, chunk),
-        out_shape=(
-            jax.ShapeDtypeStruct(queries.shape, BF16),
-            jax.ShapeDtypeStruct(key_heads.shape, BF16),
-            jax.ShapeDtypeStruct(value_heads.shape, BF16),
-            jax.ShapeDtypeStruct((side, 8), F32),
-        ),
-        in_specs=[pl.BlockSpec(memory_space=pltpu.SMEM)] + [vmem] * 5,
+        out_shape=shapes,
+        in_specs=[hbm] * 6,
         out_specs=(vmem,) * 4,
         scratch_shapes=scratch,
         compiler_params=pltpu.CompilerParams(
             collective_id=0, has_side_effects=True, vmem_limit_bytes=48 * 1024 * 1024),
-    )(sink_logits, queries, key_heads, value_heads, out_grad, segment.reshape(1, tok))
-    return query_grad, key_grad, value_grad, sink[:, :GROUPS].reshape(-1)
+    )(*[pltpu.with_memory_space_constraint(a, pltpu.HBM) for a in (sink_logits, queries, key_heads, value_heads, out_grad, segment.reshape(1, tok))])
+    query_grad, key_grad, value_grad, sink = pl.pallas_call(
+        write_out,
+        out_shape=shapes,
+        in_specs=[vmem] * 4,
+        out_specs=(hbm,) * 4,
+        scratch_shapes=[dma((4,))],
+        compiler_params=pltpu.CompilerParams(vmem_limit_bytes=1024 * 1024),
+    )(*results)
+    return query_grad, key_grad, value_grad, sink.reshape(-1)
 
 
 def solution(mesh):

time: 64.6 us -> 59.2 us (0.916)
  local copies, waits for them, and re-layouts: 7.24 us -> 0 us
  Pallas kernels: 56.5 us -> 58.4 us
    unnamed x15 -> x0, local copies, waits for them, and re-layouts: 6.65 us -> none
    pallas_call x1 -> x2, Pallas kernels: 56.5 us -> 58.4 us  [the longest x1 57.5 us: per_device(): pl.pallas_call(functools.partial(kernel, planes, chunk), out_shape=shapes...]
where the time goes in v2:
time: 59.2 us; the launch traced here: 59 us
  Pallas kernels  58.4 us (99%)
  between operations  0.64 us (1%)
    pallas_call x1, Pallas kernels, per_device(): pl.pallas_call(functools.partial(kernel, planes, chunk), out_shape=shapes...  57.5 us

profile of v2, /device:TPU:0, one launch (start us, length us, event | category | flops | bytes accessed | tf_op | source)
XLA Modules:
  0.0 59.0 jit_solution(3835972518469384874)
XLA Ops:
  0.6 57.5 %shard_map.93 = (bf16[128,2048]{1,0:T(8,128)(2,1)S(1)}, bf16[128,512]{1,0:T(8,128)(2,1)S(1)}, bf16[128,512]{1,0:T(8,128)(2,1)S(1)}, f32[1,32]{1,0:T(1,128)S(1)}) custom-call(f32[32]{0:T(128)} %sink_hbm.1, bf16[128,2048]{1,0:T(8,128)(2,1)} %q_ref.1, bf16[128,512]{1,0:T(8,128)(2,1)} %k_hbm.1, bf16[128,512]{1,0:T(8,128)(2,1)} %v_hbm.1, ...), custom_call_target="tpu_custom_call" | custom-call | tf_op jit(solution)/shard_map/pallas_call | solution.py:426
  58.1 0.9 %shard_map.94 = (bf16[128,2048]{1,0:T(8,128)(2,1)}, bf16[128,512]{1,0:T(8,128)(2,1)}, bf16[128,512]{1,0:T(8,128)(2,1)}, f32[1,32]{1,0:T(1,128)}) custom-call(bf16[128,2048]{1,0:T(8,128)(2,1)S(1)} %get-tuple-element.12.refs_0_, bf16[128,512]{1,0:T(8,128)(2,1)S(1)} %get-tuple-element.13.refs_1_, bf16[128,512]{1,0:T(8,128)(2,1)S(1)} %get-tuple-element.14.refs_2_, ...), custom_call_target="tpu_custom_call" | custom-call | tf_op jit(solution)/shard_map/pallas_call | solution.py:435

commit v3 on v2

--- a/solution.py
+++ b/solution.py
@@ -142,18 +142,19 @@
         remote(kvsend.at[0], kvbuf.at[rows(j)], s_kv.at[0], r_kv.at[j], other).wait_recv()
         remote(segsend, segbuf.at[j], s_seg.at[0], r_seg.at[j], other).wait_recv()
 
-    for k in range(1, side):
-        kv_arrive(side + flip(l, k))
-
-    @pl.when(z > 0)
-    def _():
-        for k in range(side):
-            kv_arrive(k)
-
-    for j in range(2 * side):
-        block = kvbuf[j * tok:(j + 1) * tok, :].astype(F32)
-        ktbuf[:, j * tok:(j + 1) * tok] = block.T[:HEAD_DIM].astype(BF16)
-        segcol[j * tok:(j + 1) * tok, :] = jnp.broadcast_to(segbuf[j, 0:1], (tok, tok)).T
+    def turn_over(j):
+        ktbuf[:, rows(j)] = kvbuf[rows(j), :].astype(F32).T[:HEAD_DIM].astype(BF16)
+        segcol[rows(j), :] = jnp.broadcast_to(segbuf[j, 0:1], (tok, tok)).T
+
+    for k in range(side):
+        if k:
+            kv_arrive(side + flip(l, k))
+        turn_over(side + flip(l, k))
+    for k in range(side):
+        @pl.when(z > 0)
+        def _():
+            kv_arrive(flip(l, k))
+        turn_over(flip(l, k))
 
     for copy in inputs[3:]:
         copy.wait()
@@ -162,7 +163,7 @@
     zero = jnp.zeros((tok, HEAD_DIM), BF16)
 
     def qg_back(k):
-        b = flip(l, k)
+        b = turn(l, k, side)
         return remote(qgs.at[b], oq_ref.at[:, head_cols(l)], s_qg.at[b], r_qg.at[l], base + b)
 
     lane = lax.broadcasted_iota(jnp.int32, (chunk, tok), 1)
@@ -171,7 +172,7 @@
     empty = jnp.zeros((8, lanes), F32)
 
     def prepare(k, slot):
-        b = flip(l, k)
+        b = turn(l, k, side)
         q = (qbuf[b].astype(F32) * 0.125).astype(BF16)
         g = gbuf[b]
         for h in range(GROUPS):
@@ -180,12 +181,12 @@
             rhs[slot, lanes + h * tok:lanes + (h + 1) * tok, :] = jnp.concatenate([zero, g[:, part]], 1)
 
     def arrive(k):
-        b = flip(l, k)
+        b = turn(l, k, side)
         remote(q_ref.at[:, head_cols(0)], qbuf.at[b], s_q.at[0], r_q.at[b], other).wait_recv()
         remote(g_ref.at[:, head_cols(0)], gbuf.at[b], s_g.at[0], r_g.at[b], other).wait_recv()
 
     def scores(c, k, slot, top):
-        b = flip(l, k)
+        b = turn(l, k, side)
         seg_row = segbuf[side + b, 0:1, :]
         first = pl.multiple_of(c * chunk, chunk)
         at = pl.ds(pl.multiple_of(b * tok + c * chunk, tok), chunk)
@@ -211,8 +212,15 @@
         mixed = mixed + jnp.sum((e * dp).reshape(chunk // 8, 8, lanes), 0)
         return total, mixed
 
+    def kg_prev(k):
+        d = turn(l, k, side)
+        return remote(kvgs.at[d], kvnx.at[l], s_kg.at[k], r_kg.at[l], base - side + d)
+
+    def sink_to(p):
+        return remote(sinksum, sinkplanes.at[z], s_sa.at[p], r_sa.at[z], p * side + l)
+
     def step(k, top, last):
-        b = flip(l, k)
+        b = turn(l, k, side)
         slot = k % 2
         start = pl.multiple_of(b * tok, tok)
         top = jnp.max(top, 0, keepdims=True)
@@ -236,10 +244,22 @@
         delta = jnp.sum(mixed, 0, keepdims=True) * inv
         sinkacc[...] = sinkacc[...] - jnp.broadcast_to(sink_exp * inv * delta, sinkacc.shape)
 
+        if last:
+            for h in range(GROUPS):
+                sinksum[h:h + 1, :] = sinkacc[0:1, h * tok:(h + 1) * tok]
+            sinksum[GROUPS:, :] = jnp.zeros((8 - GROUPS, tok), F32)
+            sinkplanes[z] = sinksum[...]
+
         for h in range(GROUPS):
             inv_col = jnp.broadcast_to(inv[:, h * tok:(h + 1) * tok], (tok, tok)).T
             for r in (h * tok, lanes + h * tok):
                 grhs[r:r + tok, :] = (rhs[slot, r:r + tok, :].astype(F32) * inv_col).astype(BF16)
+
+        if last:
+            for p in range(planes):
+                @pl.when(p != z)
+                def _():
+                    sink_to(p).start()
 
         def grads(c, qgt):
             first = pl.multiple_of(c * chunk, chunk)
@@ -252,6 +272,7 @@
                                  preferred_element_type=F32)
 
         qgt = lax.fori_loop(0, span // chunk, grads, jnp.zeros((HEAD_DIM, lanes), F32))
+        kvgs[b] = acc[rows(b), :].astype(BF16)
         qgt = qgt * (inv * 0.125)
         for pair in range(GROUPS // 2):
             two = jnp.concatenate(
@@ -261,6 +282,10 @@
         @pl.when(k > 0)
         def _():
             qg_back(k).start()
+
+        @pl.when((k > 1) & (z > 0))
+        def _():
+            kg_prev(k).start()
         return ahead
 
     prepare(0, 0)
@@ -268,35 +293,21 @@
     top = lax.fori_loop(0, side - 1, lambda k, t: step(k, t, False), top)
     step(side - 1, top, True)
 
-    for j in range(2 * side):
+    for j in (l, flip(l, 1)):
+        kvgs[j] = acc[rows(j), :].astype(BF16)
+    for j in range(side, 2 * side):
         kvgs[j] = acc[j * tok:(j + 1) * tok, :].astype(BF16)
-    for h in range(GROUPS):
-        sinksum[h:h + 1, :] = sinkacc[0:1, h * tok:(h + 1) * tok]
-    sinksum[GROUPS:, :] = jnp.zeros((8 - GROUPS, tok), F32)
     oq_ref[:, head_cols(l)] = qgs[l]
     kvin[l] = kvgs[side + l]
-    sinkplanes[z] = sinksum[...]
-
-    def kg_prev(k):
-        d = flip(l, k)
-        return remote(kvgs.at[d], kvnx.at[l], s_kg.at[k], r_kg.at[l], base - side + d)
 
     def kg_own(k):
         d = flip(l, k)
         return remote(kvgs.at[side + d], kvin.at[l], s_kg.at[side + k], r_kg.at[side + l], base + d)
 
-    def sink_to(p):
-        return remote(sinksum, sinkplanes.at[z], s_sa.at[p], r_sa.at[z], p * side + l)
-
     @pl.when(z > 0)
     def _():
-        for k in range(side):
-            kg_prev(k).start()
-
-    for p in range(planes):
-        @pl.when(p != z)
-        def _():
-            sink_to(p).start()
+        kg_prev(0).start()
+        kg_prev(1).start()
 
     for k in range(1, side):
         kg_own(k).start()
@@ -363,6 +374,15 @@
     for k in range(1, side):
         for copy in kv_own(k) + qg_to(k) + (qg_back(k), kg_own(k), sink_side(k)):
             copy.wait_send()
+
+
+def turn(l, k, side):
+    pairs = side // 2
+    pair = k // 2
+    later = (pair + pairs - 1) // pairs
+    own = l + (k % 2) * (1 - 2 * (l % 2))
+    other = pair - 1 + (pair - 1 - l // 2 + pairs) // pairs
+    return (1 - later) * own + later * (2 * other + k % 2)
 
 
 def write_out(*refs):

time: 59.2 us -> 57.4 us (0.970); the launches traced: 59 us -> 56.4 us
  Pallas kernels: 58.4 us -> 55.8 us
    pallas_call x1, Pallas kernels: 57.5 us -> 54.8 us  [per_device(): pl.pallas_call(functools.partial(kernel, planes, chunk), out_shape=shapes...]
where the time goes in v3:
time: 57.4 us; the launch traced here: 56.4 us
  Pallas kernels  55.8 us (97%)
  between operations  0.64 us (1%)
    pallas_call x1, Pallas kernels, per_device(): pl.pallas_call(functools.partial(kernel, planes, chunk), out_shape=shapes...  54.8 us

profile of v3, /device:TPU:0, one launch (start us, length us, event | category | flops | bytes accessed | tf_op | source)
XLA Modules:
  0.0 56.4 jit_solution(6816293974121460633)
XLA Ops:
  0.6 54.8 %shard_map.93 = (bf16[128,2048]{1,0:T(8,128)(2,1)S(1)}, bf16[128,512]{1,0:T(8,128)(2,1)S(1)}, bf16[128,512]{1,0:T(8,128)(2,1)S(1)}, f32[1,32]{1,0:T(1,128)S(1)}) custom-call(f32[32]{0:T(128)} %sink_hbm.1, bf16[128,2048]{1,0:T(8,128)(2,1)} %q_ref.1, bf16[128,512]{1,0:T(8,128)(2,1)} %k_hbm.1, bf16[128,512]{1,0:T(8,128)(2,1)} %v_hbm.1, ...), custom_call_target="tpu_custom_call" | custom-call | tf_op jit(solution)/shard_map/pallas_call | solution.py:446
  55.5 0.9 %shard_map.94 = (bf16[128,2048]{1,0:T(8,128)(2,1)}, bf16[128,512]{1,0:T(8,128)(2,1)}, bf16[128,512]{1,0:T(8,128)(2,1)}, f32[1,32]{1,0:T(1,128)}) custom-call(bf16[128,2048]{1,0:T(8,128)(2,1)S(1)} %get-tuple-element.12.refs_0_, bf16[128,512]{1,0:T(8,128)(2,1)S(1)} %get-tuple-element.13.refs_1_, bf16[128,512]{1,0:T(8,128)(2,1)S(1)} %get-tuple-element.14.refs_2_, ...), custom_call_target="tpu_custom_call" | custom-call | tf_op jit(solution)/shard_map/pallas_call | solution.py:455
